TPU v7x, 256 devices: a whole 4x4x8 slice. The times are simulated.
256 devices in a mesh: gx: 4 (over y), gy: 16 (over z, core), gz: 4 (over x).
Axes of the slice: x: 4, y: 4, z: 8, core: 2. Of those that a mesh axis runs over, the one named last changes fastest.
Arguments:
- field: bfloat16 [16, 64, 256, 512], P(None, 'gz', 'gy', 'gx'), may hold values from -6 to 6
- fine_taps: float32 [3, 9], replicated, may hold values from 0.1 to 0.6
- coarse_taps: float32 [3, 9], replicated, may hold values from 0.1 to 0.6
- top_kernel: bfloat16 [8, 32, 64, 16384], P('gz', 'gy', 'gx'), may hold values from -4 to 4
Outputs:
- applied: bfloat16 [16, 64, 256, 512], P(None, 'gz', 'gy', 'gx')
All inputs are finite; a program needn't handle non-finite values.
Results may differ from a plain program's by a relative error of at most 0.0047.
Values may be sent and summed in bfloat16 or wider, within the bound.
A program may use at most 128 MiB of HBM per device.

v0:
```python
import jax
import jax.numpy as jnp
from jax import lax
from jax.sharding import PartitionSpec as P


def padded_2(cells, sides, width):
    for axis, dim in sides:
        count = lax.axis_size(axis)
        ends = count - 1
        head = lax.slice_in_dim(cells, 0, width, axis=dim)
        tail = lax.slice_in_dim(cells, cells.shape[dim] - width, cells.shape[dim], axis=dim)
        cells = jnp.concatenate(
            [
                lax.ppermute(tail, axis, [(i, (i + 1) % count) for i in range(ends)]),
                cells,
                lax.ppermute(head, axis, [((i + 1) % count, i) for i in range(ends)]),
            ],
            axis=dim,
        )
    return cells


def in_order(blocks, dim):
    shape = list(blocks.shape[1:])
    shape[dim] *= blocks.shape[0]
    return jnp.moveaxis(blocks, 0, dim).reshape(shape)


def copy_for_each(shard, axis):
    devices = lax.axis_size(axis)
    return lax.all_to_all(
        jnp.broadcast_to(shard[None], (devices, *shard.shape)), axis, 0, 0, tiled=True
    )


def gather_directly(shard, axis, dim):
    return in_order(copy_for_each(shard, axis), dim)


def band_matrix(kernel_row, padded_length):
    length = padded_length - 8
    source = lax.broadcasted_iota(jnp.int32, (padded_length, length), 0)
    target = lax.broadcasted_iota(jnp.int32, (padded_length, length), 1)
    offset = source - target
    band = jnp.zeros((padded_length, length), jnp.float32)
    for tap in range(9):
        band = band + jnp.where(offset == tap, kernel_row[tap], 0.0)
    return band


def conv_padded(padded, kernel_row, along):
    length = padded.shape[along] - 8
    if along == padded.ndim - 1:
        band = band_matrix(kernel_row, padded.shape[along])
        return lax.dot_general(
            padded,
            band,
            (((along,), (0,)), ((), ())),
            precision=lax.Precision.HIGHEST,
            preferred_element_type=jnp.float32,
        )
    total = kernel_row[0] * lax.slice_in_dim(padded, 0, length, axis=along)
    for offset in range(1, 9):
        total = total + kernel_row[offset] * lax.slice_in_dim(
            padded, offset, offset + length, axis=along
        )
    return total


def separable_box(padded, kernel):
    values = conv_padded(padded.astype(jnp.float32), kernel[2], 3)
    values = conv_padded(values, kernel[1], 2)
    return conv_padded(values, kernel[0], 1)


def restrict(values, factor):
    count, depth, rows, cols = values.shape
    shaped = values.reshape(
        count, depth // factor, factor, rows // factor, factor, cols // factor, factor
    )
    return shaped.mean(axis=(2, 4, 6))


def prolong(values, factor):
    values = jnp.repeat(values, factor, axis=1)
    values = jnp.repeat(values, factor, axis=2)
    return jnp.repeat(values, factor, axis=3)


def shards(field, fine_taps, coarse_taps, top_kernel):
    cells = field.astype(jnp.float32)
    coarse_cells = restrict(cells, 2)
    fine_padded = padded_2(field, (("gx", 3), ("gy", 2), ("gz", 1)), 4)
    coarse_padded = padded_2(
        coarse_cells.astype(jnp.bfloat16), (("gx", 3), ("gy", 2), ("gz", 1)), 4
    ).astype(coarse_cells.dtype)
    fine_part = separable_box(fine_padded, fine_taps)
    coarse_part = separable_box(coarse_padded, coarse_taps)
    top_in = restrict(coarse_cells, 4).astype(jnp.bfloat16)
    count, top_depth, top_rows, top_cols = top_in.shape
    along_x = gather_directly(top_in, "gx", 3)
    along_y = gather_directly(along_x, "gy", 2)
    along_z = gather_directly(along_y, "gz", 1)
    whole_top = along_z.reshape(count, -1)
    kernel_rows = top_kernel.reshape(-1, top_kernel.shape[3])
    top_part = lax.dot_general(
        whole_top, kernel_rows, (((1,), (1,)), ((), ())), preferred_element_type=jnp.float32
    )
    top_part = top_part.reshape(count, top_depth, top_rows, top_cols)
    coarse_total = coarse_part + prolong(top_part, 4)
    return (fine_part + prolong(coarse_total, 2)).astype(jnp.bfloat16)


def solution(mesh):
    return jax.shard_map(
        shards,
        mesh=mesh,
        in_specs=(P(None, "gz", "gy", "gx"), P(), P(), P("gz", "gy", "gx", None)),
        out_specs=P(None, "gz", "gy", "gx"),
        check_vma=False,
    )
```

profile of v0, /device:TPU:1, one launch (start us, length us, event | category | flops | bytes accessed | tf_op | source)
XLA Modules:
  0.0 229.9 jit_solution(6586776564835972903)
XLA Ops:
  0.0 10.1 %copy.37 = f32[16,16,16,128]{0,3,2,1:T(8,128)} copy(bf16[16,16,16,128]{3,2,1,0:T(8,128)(2,1)} %param.4) | data formatting | bytes 3145728 | tf_op jit(solution)/shard_map/reshape | solution.py:79
  10.1 13.1 %reduce_sum.18 = f32[16,8,8,64]{0,3,2,1:T(8,128)} reduce(f32[16,8,2,8,2,64,2]{0,6,5,4,3,2,1:T(2,128)} %bitcast.84, f32[]{:T(128)} %constant.13.clone.1), dimensions={2,4,6}, to_apply=%region_0.0 | reduce | flops 458752 | bytes 2359300 | tf_op jit(solution)/shard_map/reduce_sum | solution.py:82
  30.7 5.0 %all-to-all-start = ((bf16[4,2,512]{2,1,0:T(2,128)(2,1)}), bf16[4,2,512]{2,1,0:T(2,128)(2,1)S(1)}, u32[]{:S(2)}, u32[]{:S(2)}) async-start(bf16[4,2,512]{2,1,0:T(2,128)(2,1)} %reshape.161), calls=%async_computation | async-start | bytes 16384 | tf_op jit(solution)/shard_map/all_to_all | solution.py:32
  37.9 4.7 %collective-permute-start.6 = (bf16[16,8,8,4]{3,2,1,0:T(8,128)(2,1)}, bf16[16,8,8,4]{3,2,1,0:T(8,128)(2,1)}, u32[]{:S(2)}, u32[]{:S(2)}) collective-permute-start(bf16[16,8,8,4]{3,2,1,0:T(8,128)(2,1)} %get-tuple-element.17), channel_id=1, source_target_pairs={{0,64},{64,128},{128,192},{1,65},{65,129},{129,193},{2,66},{66,130... | collective-permute-start | bytes 24584 | tf_op jit(solution)/shard_map/ppermute | solution.py:15
  44.4 3.7 %copy.57 = bf16[16,16,16,4]{2,1,3,0:T(8,128)(2,1)} copy(bf16[16,16,16,4]{3,2,1,0:T(8,128)(2,1)} %get-tuple-element.10) | data formatting | bytes 65536
  49.4 3.6 %copy.56 = bf16[16,16,16,4]{2,1,3,0:T(8,128)(2,1)} copy(bf16[16,16,16,4]{3,2,1,0:T(8,128)(2,1)} %get-tuple-element.9) | data formatting | bytes 65536
  53.0 4.7 %collective-permute-start = (bf16[16,16,16,4]{2,1,3,0:T(8,128)(2,1)}, bf16[16,16,16,4]{2,1,3,0:T(8,128)(2,1)}, u32[]{:S(2)}, u32[]{:S(2)}) collective-permute-start(bf16[16,16,16,4]{2,1,3,0:T(8,128)(2,1)} %copy.56), channel_id=1, source_target_pairs={{0,64},{64,128},{128,192},{1,65},{65,129},{129,193},{2,66},{66,130... | collective-permute-start | bytes 98312 | tf_op jit(solution)/shard_map/ppermute | solution.py:15
  60.6 4.4 %collective-permute-start.9 = (bf16[16,8,4,72]{3,2,1,0:T(4,128)(2,1)S(1)}, bf16[16,8,4,72]{3,2,1,0:T(4,128)(2,1)S(1)}, u32[]{:S(2)}, u32[]{:S(2)}) collective-permute-start(bf16[16,8,4,72]{3,2,1,0:T(4,128)(2,1)S(1)} %get-tuple-element.16), channel_id=1, source_target_pairs={{4,0},{8,4},{12,8},{16,12},{20,16},{24,20},{28,24},{32,28},{36,32}... | collective-permute-start | bytes 221192 | tf_op jit(solution)/shard_map/ppermute | solution.py:17
  74.0 4.7 %collective-permute-start.10 = (bf16[16,4,16,72]{3,2,1,0:T(8,128)(2,1)}, bf16[16,4,16,72]{3,2,1,0:T(8,128)(2,1)}, u32[]{:S(2)}, u32[]{:S(2)}) collective-permute-start(bf16[16,4,16,72]{3,2,1,0:T(8,128)(2,1)} %get-tuple-element.11), channel_id=1, source_target_pairs={{0,1},{1,2},{2,3},{4,5},{5,6},{6,7},{8,9},{9,10},{10,11},{12,13},{... | collective-permute-start | bytes 442376 | tf_op jit(solution)/shard_map/ppermute | solution.py:15
  82.4 11.2 %all-to-all-start.1 = ((bf16[16,2,2048]{2,1,0:T(2,128)(2,1)}), bf16[16,2,2048]{2,1,0:T(2,128)(2,1)S(1)}, u32[]{:S(2)}, u32[]{:S(2)}) async-start(bf16[16,2,2048]{2,1,0:T(2,128)(2,1)} %reshape.163), calls=%async_computation.1 | async-start | bytes 262144 | tf_op jit(solution)/shard_map/all_to_all | solution.py:32
  100.6 4.1 %pad_maximum_fusion.7 = (bf16[16,16,4,136]{3,2,1,0:T(4,128)(2,1)}, bf16[16,16,4,136]{3,2,1,0:T(4,128)(2,1)}) fusion(bf16[16,16,16,4]{3,2,1,0:T(8,128)(2,1)} %copy.36, bf16[16,16,16,128]{3,2,1,0:T(8,128)(2,1)S(1)} %copy-done.2, bf16[16,16,16,4]{3,2,1,0:T(8,128)(2,1)} %copy.35), kind=kLoop, calls=%fused_computation.106 | loop fusion | flops 1671168 | bytes 1671168 | tf_op jit(solution)/shard_map/slice | solution.py:12
  106.7 3.7 %collective-permute-start.2 = (bf16[16,16,4,136]{3,2,1,0:T(4,128)(2,1)}, bf16[16,16,4,136]{3,2,1,0:T(4,128)(2,1)}, u32[]{:S(2)}, u32[]{:S(2)}) collective-permute-start(bf16[16,16,4,136]{3,2,1,0:T(4,128)(2,1)} %get-tuple-element.7), channel_id=1, source_target_pairs={{0,4},{4,8},{8,12},{12,16},{16,20},{20,24},{24,28},{28,32},{32,36}... | collective-permute-start | bytes 835592 | tf_op jit(solution)/shard_map/ppermute | solution.py:15
  110.5 9.6 %fusion.40 = f32[16,16,16,64]{3,2,1,0:T(8,128)} fusion(bf16[16,4,16,72]{3,2,1,0:T(8,128)(2,1)} %collective-permute-done.11, bf16[16,8,4,72]{3,2,1,0:T(4,128)(2,1)S(1)} %copy-done.11, bf16[16,8,8,4]{3,2,1,0:T(8,128)(2,1)} %collective-permute-done.7, bf16[16,8,8,64]{3,2,1,0:T(8,128)(2,1)S(1)} %get-tuple-element.13, ...), kind=kOutput, calls=%fused_computation.67 | convolution fusion | flops 230745600 | bytes 1638436 | tf_op jit(solution)/shard_map/dot_general | solution.py:56
  122.2 4.1 %all-to-all-start.2 = ((bf16[4,2,32768]{2,1,0:T(2,128)(2,1)}), bf16[4,2,32768]{2,1,0:T(2,128)(2,1)}, u32[]{:S(2)}, u32[]{:S(2)}) async-start(bf16[4,2,32768]{2,1,0:T(2,128)(2,1)} %reshape.165), calls=%async_computation.2 | async-start | bytes 1048576 | tf_op jit(solution)/shard_map/all_to_all | solution.py:32
  126.4 13.8 %fusion.32 = f32[16,16,8,64]{3,2,1,0:T(8,128)S(1)} fusion(f32[16,16,16,64]{3,2,1,0:T(8,128)} %fusion.40, f32[]{:T(128)} %bitcast.50, f32[]{:T(128)} %bitcast.49, f32[]{:T(128)} %bitcast.48, f32[]{:T(128)} %bitcast.47, f32[]{:T(128)} %bitcast.46, f32[]{:T(128)} %bitcast.45, f32[]{:T(128)} %bitcast.44, f32[]{:T(128)} %bitcast.43, f32[]{:T(128)} %bitcast.30), kind=kLoop, calls=%fused_computation.51 | loop fusion | flops 2228224 | bytes 5242916 | tf_op jit(solution)/shard_map/add | solution.py:65
  140.2 3.9 %pad_maximum_fusion.4 = (bf16[16,4,24,136]{3,2,1,0:T(8,128)(2,1)}, bf16[16,4,24,136]{3,2,1,0:T(8,128)(2,1)}) fusion(bf16[16,16,4,136]{3,2,1,0:T(4,128)(2,1)} %collective-permute-done.3, bf16[16,16,4,136]{3,2,1,0:T(4,128)(2,1)} %collective-permute-done.2, bf16[16,16,16,4]{3,2,1,0:T(8,128)(2,1)S(1)} %copy-done.5, bf16[16,16,16,128]{3,2,1,0:T(8,128)(2,1)S(1)} %copy-done.3, ...), kind=kLoop, calls=%fused_computation.85 | loop fusion | flops 4177920 | bytes 2506752 | tf_op jit(solution)/shard_map/slice | solution.py:12
  145.5 4.9 %collective-permute-start.4 = (bf16[16,4,24,136]{3,2,1,0:T(8,128)(2,1)}, bf16[16,4,24,136]{3,2,1,0:T(8,128)(2,1)}, u32[]{:S(2)}, u32[]{:S(2)}) collective-permute-start(bf16[16,4,24,136]{3,2,1,0:T(8,128)(2,1)} %get-tuple-element.5), channel_id=1, source_target_pairs={{0,1},{1,2},{2,3},{4,5},{5,6},{6,7},{8,9},{9,10},{10,11},{12,13},{... | collective-permute-start | bytes 1253384 | tf_op jit(solution)/shard_map/ppermute | solution.py:15
  163.6 6.8 %fusion.55 = f32[16,8,8,64]{3,2,1,0:T(8,128)S(1)} fusion(f32[16,8,8,64]{3,2,1,0:T(8,128)} %copy.47, f32[16,16,8,64]{3,2,1,0:T(8,128)S(1)} %fusion.32, f32[]{:T(128)} %bitcast.58, f32[]{:T(128)} %bitcast.57, f32[]{:T(128)} %bitcast.56, f32[]{:T(128)} %bitcast.55, f32[]{:T(128)} %bitcast.54, f32[]{:T(128)} %bitcast.53, f32[]{:T(128)} %bitcast.52, f32[]{:T(128)} %bitcast.51, ...), kind=kLoop, calls=%fused_computation.88 | loop fusion | flops 1179648 | bytes 2883620 | tf_op jit(solution)/shard_map/add | solution.py:111
  171.1 5.4 %copy.49 = f32[16,16,16,64]{2,1,3,0:T(8,128)} copy(f32[16,16,16,64]{3,1,2,0:T(8,128)S(1)} %bitcast.87) | data formatting | bytes 2097152 | tf_op jit(solution)/shard_map/reshape | solution.py:87
  176.4 10.7 %broadcast_in_dim.148 = f32[16,16,16,64,2]{2,1,4,3,0:T(8,128)} broadcast(f32[16,16,16,64]{2,1,3,0:T(8,128)} %copy.49), dimensions={0,1,2,3} | broadcast | bytes 3145728 | tf_op jit(solution)/shard_map/broadcast_in_dim | solution.py:88
  187.1 11.6 %copy.50 = f32[16,16,16,128]{3,2,1,0:T(8,128)} copy(f32[16,16,16,128]{2,1,3,0:T(8,128)} %bitcast.83) | data formatting | bytes 4194304 | tf_op jit(solution)/shard_map/reshape | solution.py:88
  198.7 13.4 %fusion = f32[16,24,24,128]{3,2,1,0:T(8,128)S(1)} fusion(bf16[16,4,24,136]{3,2,1,0:T(8,128)(2,1)} %collective-permute-done.5, bf16[16,16,4,136]{3,2,1,0:T(4,128)(2,1)} %collective-permute-done.3, bf16[16,16,16,4]{3,2,1,0:T(8,128)(2,1)S(1)} %copy-done.6, bf16[16,16,16,128]{3,2,1,0:T(8,128)(2,1)S(1)} %copy-done.4, bf16[16,16,16,4]{3,2,1,0:T(8,128)(2,1)S(1)} %copy-done.8, ...), kind=kOutput, calls=%fused_computation | convolution fusion | flops 1943202816 | bytes 7225380 | tf_op jit(solution)/shard_map/dot_general | solution.py:56
  212.2 8.9 %fusion.14 = f32[16,24,16,128]{3,2,1,0:T(8,128)S(1)} fusion(f32[16,24,24,128]{3,2,1,0:T(8,128)S(1)} %fusion, f32[]{:T(128)} %bitcast.20, f32[]{:T(128)} %bitcast.19, f32[]{:T(128)} %bitcast.18, f32[]{:T(128)} %bitcast.17, f32[]{:T(128)} %bitcast.16, f32[]{:T(128)} %bitcast.15, f32[]{:T(128)} %bitcast.14, f32[]{:T(128)} %bitcast.13, f32[]{:T(128)} %bitcast.1), kind=kLoop, calls=%fused_computation.15 | loop fusion | flops 13369344 | bytes 31457316 | tf_op jit(solution)/shard_map/add | solution.py:65
  221.0 8.8 %fusion.24 = bf16[16,16,16,128]{3,2,1,0:T(8,128)(2,1)} fusion(f32[16,16,16,128]{3,2,1,0:T(8,128)S(1)} %copy-done.9, f32[16,24,16,128]{3,2,1,0:T(8,128)S(1)} %fusion.14, f32[]{:T(128)} %bitcast.28, f32[]{:T(128)} %bitcast.27, f32[]{:T(128)} %bitcast.26, f32[]{:T(128)} %bitcast.25, f32[]{:T(128)} %bitcast.24, f32[]{:T(128)} %bitcast.23, f32[]{:T(128)} %bitcast.22, ...), kind=kLoop, calls=%fused_computation.34 | loop fusion | flops 9961472 | bytes 22020132 | tf_op jit(solution)/shard_map/convert_element_type | solution.py:112
  (95 shorter events, 54.5 us)
Async XLA Ops:
  0.0 158.0 %copy-start = (bf16[2,2,16,16384]{3,2,1,0:T(8,128)(2,1)S(1)}, bf16[2,2,16,16384]{3,2,1,0:T(8,128)(2,1)}, u32[]{:S(2)}) copy-start(bf16[2,2,16,16384]{3,2,1,0:T(8,128)(2,1)} %param.7) | copy-start | bytes 6291460
  27.6 15.0 %copy-start.2 = (bf16[16,16,16,128]{3,2,1,0:T(8,128)(2,1)S(1)}, bf16[16,16,16,128]{3,2,1,0:T(8,128)(2,1)}, u32[]{:S(2)}) copy-start(bf16[16,16,16,128]{3,2,1,0:T(8,128)(2,1)} %param.4) | copy-start | bytes 3145732
  30.7 48.7 %all-to-all-start = ((bf16[4,2,512]{2,1,0:T(2,128)(2,1)}), bf16[4,2,512]{2,1,0:T(2,128)(2,1)S(1)}, u32[]{:S(2)}, u32[]{:S(2)}) async-start(bf16[4,2,512]{2,1,0:T(2,128)(2,1)} %reshape.161), calls=%async_computation | async-start | bytes 16384 | tf_op jit(solution)/shard_map/all_to_all | solution.py:32
  36.6 22.6 %collective-permute-start.7 = (bf16[16,8,8,4]{3,2,1,0:T(8,128)(2,1)}, bf16[16,8,8,4]{3,2,1,0:T(8,128)(2,1)}, u32[]{:S(2)}, u32[]{:S(2)}) collective-permute-start(bf16[16,8,8,4]{3,2,1,0:T(8,128)(2,1)} %get-tuple-element.18), channel_id=1, source_target_pairs={{64,0},{128,64},{192,128},{65,1},{129,65},{193,129},{66,2},{130,66... | collective-permute-start | bytes 24584 | tf_op jit(solution)/shard_map/ppermute | solution.py:17
  37.9 21.3 %collective-permute-start.6 = (bf16[16,8,8,4]{3,2,1,0:T(8,128)(2,1)}, bf16[16,8,8,4]{3,2,1,0:T(8,128)(2,1)}, u32[]{:S(2)}, u32[]{:S(2)}) collective-permute-start(bf16[16,8,8,4]{3,2,1,0:T(8,128)(2,1)} %get-tuple-element.17), channel_id=1, source_target_pairs={{0,64},{64,128},{128,192},{1,65},{65,129},{129,193},{2,66},{66,130... | collective-permute-start | bytes 24584 | tf_op jit(solution)/shard_map/ppermute | solution.py:15
  44.4 13.3 %copy-start.14 = (f32[3,9]{1,0:T(4,128)S(1)}, f32[3,9]{1,0:T(4,128)}, u32[]{:S(2)}) copy-start(f32[3,9]{1,0:T(4,128)} %param.6) | copy-start | bytes 328
  44.4 14.0 %copy-start.15 = (f32[3,9]{1,0:T(4,128)S(1)}, f32[3,9]{1,0:T(4,128)}, u32[]{:S(2)}) copy-start(f32[3,9]{1,0:T(4,128)} %param.5) | copy-start | bytes 328
  48.1 45.4 %collective-permute-start.1 = (bf16[16,16,16,4]{2,1,3,0:T(8,128)(2,1)}, bf16[16,16,16,4]{2,1,3,0:T(8,128)(2,1)}, u32[]{:S(2)}, u32[]{:S(2)}) collective-permute-start(bf16[16,16,16,4]{2,1,3,0:T(8,128)(2,1)} %copy.57), channel_id=1, source_target_pairs={{64,0},{128,64},{192,128},{65,1},{129,65},{193,129},{66,2},{130,66... | collective-permute-start | bytes 98312 | tf_op jit(solution)/shard_map/ppermute | solution.py:17
  53.0 44.0 %collective-permute-start = (bf16[16,16,16,4]{2,1,3,0:T(8,128)(2,1)}, bf16[16,16,16,4]{2,1,3,0:T(8,128)(2,1)}, u32[]{:S(2)}, u32[]{:S(2)}) collective-permute-start(bf16[16,16,16,4]{2,1,3,0:T(8,128)(2,1)} %copy.56), channel_id=1, source_target_pairs={{0,64},{64,128},{128,192},{1,65},{65,129},{129,193},{2,66},{66,130... | collective-permute-start | bytes 98312 | tf_op jit(solution)/shard_map/ppermute | solution.py:15
  60.6 8.2 %collective-permute-start.9 = (bf16[16,8,4,72]{3,2,1,0:T(4,128)(2,1)S(1)}, bf16[16,8,4,72]{3,2,1,0:T(4,128)(2,1)S(1)}, u32[]{:S(2)}, u32[]{:S(2)}) collective-permute-start(bf16[16,8,4,72]{3,2,1,0:T(4,128)(2,1)S(1)} %get-tuple-element.16), channel_id=1, source_target_pairs={{4,0},{8,4},{12,8},{16,12},{20,16},{24,20},{28,24},{32,28},{36,32}... | collective-permute-start | bytes 221192 | tf_op jit(solution)/shard_map/ppermute | solution.py:17
  65.0 4.9 %collective-permute-start.8 = (bf16[16,8,4,72]{3,2,1,0:T(4,128)(2,1)S(1)}, bf16[16,8,4,72]{3,2,1,0:T(4,128)(2,1)S(1)}, u32[]{:S(2)}, u32[]{:S(2)}) collective-permute-start(bf16[16,8,4,72]{3,2,1,0:T(4,128)(2,1)S(1)} %get-tuple-element.15), channel_id=1, source_target_pairs={{0,4},{4,8},{8,12},{12,16},{16,20},{20,24},{24,28},{28,32},{32,36}... | collective-permute-start | bytes 221192 | tf_op jit(solution)/shard_map/ppermute | solution.py:15
  72.7 37.7 %collective-permute-start.11 = (bf16[16,4,16,72]{3,2,1,0:T(8,128)(2,1)}, bf16[16,4,16,72]{3,2,1,0:T(8,128)(2,1)}, u32[]{:S(2)}, u32[]{:S(2)}) collective-permute-start(bf16[16,4,16,72]{3,2,1,0:T(8,128)(2,1)} %get-tuple-element.12), channel_id=1, source_target_pairs={{1,0},{2,1},{3,2},{5,4},{6,5},{7,6},{9,8},{10,9},{11,10},{13,12},{... | collective-permute-start | bytes 442376 | tf_op jit(solution)/shard_map/ppermute | solution.py:17
  74.0 36.5 %collective-permute-start.10 = (bf16[16,4,16,72]{3,2,1,0:T(8,128)(2,1)}, bf16[16,4,16,72]{3,2,1,0:T(8,128)(2,1)}, u32[]{:S(2)}, u32[]{:S(2)}) collective-permute-start(bf16[16,4,16,72]{3,2,1,0:T(8,128)(2,1)} %get-tuple-element.11), channel_id=1, source_target_pairs={{0,1},{1,2},{2,3},{4,5},{5,6},{6,7},{8,9},{9,10},{10,11},{12,13},{... | collective-permute-start | bytes 442376 | tf_op jit(solution)/shard_map/ppermute | solution.py:15
  82.4 37.7 %all-to-all-start.1 = ((bf16[16,2,2048]{2,1,0:T(2,128)(2,1)}), bf16[16,2,2048]{2,1,0:T(2,128)(2,1)S(1)}, u32[]{:S(2)}, u32[]{:S(2)}) async-start(bf16[16,2,2048]{2,1,0:T(2,128)(2,1)} %reshape.163), calls=%async_computation.1 | async-start | bytes 262144 | tf_op jit(solution)/shard_map/all_to_all | solution.py:32
  104.7 35.5 %collective-permute-start.3 = (bf16[16,16,4,136]{3,2,1,0:T(4,128)(2,1)}, bf16[16,16,4,136]{3,2,1,0:T(4,128)(2,1)}, u32[]{:S(2)}, u32[]{:S(2)}) collective-permute-start(bf16[16,16,4,136]{3,2,1,0:T(4,128)(2,1)} %get-tuple-element.8), channel_id=1, source_target_pairs={{4,0},{8,4},{12,8},{16,12},{20,16},{24,20},{28,24},{32,28},{36,32}... | collective-permute-start | bytes 835592 | tf_op jit(solution)/shard_map/ppermute | solution.py:17
  106.7 33.5 %collective-permute-start.2 = (bf16[16,16,4,136]{3,2,1,0:T(4,128)(2,1)}, bf16[16,16,4,136]{3,2,1,0:T(4,128)(2,1)}, u32[]{:S(2)}, u32[]{:S(2)}) collective-permute-start(bf16[16,16,4,136]{3,2,1,0:T(4,128)(2,1)} %get-tuple-element.7), channel_id=1, source_target_pairs={{0,4},{4,8},{8,12},{12,16},{16,20},{20,24},{24,28},{28,32},{32,36}... | collective-permute-start | bytes 835592 | tf_op jit(solution)/shard_map/ppermute | solution.py:15
  122.2 28.2 %all-to-all-start.2 = ((bf16[4,2,32768]{2,1,0:T(2,128)(2,1)}), bf16[4,2,32768]{2,1,0:T(2,128)(2,1)}, u32[]{:S(2)}, u32[]{:S(2)}) async-start(bf16[4,2,32768]{2,1,0:T(2,128)(2,1)} %reshape.165), calls=%async_computation.2 | async-start | bytes 1048576 | tf_op jit(solution)/shard_map/all_to_all | solution.py:32
  126.3 13.9 %copy-start.3 = (bf16[16,16,16,128]{3,2,1,0:T(8,128)(2,1)S(1)}, bf16[16,16,16,128]{3,2,1,0:T(8,128)(2,1)}, u32[]{:S(2)}) copy-start(bf16[16,16,16,128]{3,2,1,0:T(8,128)(2,1)} %param.4) | copy-start | bytes 3145732
  126.3 13.9 %copy-start.5 = (bf16[16,16,16,4]{3,2,1,0:T(8,128)(2,1)S(1)}, bf16[16,16,16,4]{3,2,1,0:T(8,128)(2,1)}, u32[]{:S(2)}) copy-start(bf16[16,16,16,4]{3,2,1,0:T(8,128)(2,1)} %copy.36) | copy-start | bytes 98308
  126.4 13.9 %copy-start.7 = (bf16[16,16,16,4]{3,2,1,0:T(8,128)(2,1)S(1)}, bf16[16,16,16,4]{3,2,1,0:T(8,128)(2,1)}, u32[]{:S(2)}) copy-start(bf16[16,16,16,4]{3,2,1,0:T(8,128)(2,1)} %copy.35) | copy-start | bytes 98308
  144.2 54.5 %collective-permute-start.5 = (bf16[16,4,24,136]{3,2,1,0:T(8,128)(2,1)}, bf16[16,4,24,136]{3,2,1,0:T(8,128)(2,1)}, u32[]{:S(2)}, u32[]{:S(2)}) collective-permute-start(bf16[16,4,24,136]{3,2,1,0:T(8,128)(2,1)} %get-tuple-element.6), channel_id=1, source_target_pairs={{1,0},{2,1},{3,2},{5,4},{6,5},{7,6},{9,8},{10,9},{11,10},{13,12},{... | collective-permute-start | bytes 1253384 | tf_op jit(solution)/shard_map/ppermute | solution.py:17
  145.5 53.2 %collective-permute-start.4 = (bf16[16,4,24,136]{3,2,1,0:T(8,128)(2,1)}, bf16[16,4,24,136]{3,2,1,0:T(8,128)(2,1)}, u32[]{:S(2)}, u32[]{:S(2)}) collective-permute-start(bf16[16,4,24,136]{3,2,1,0:T(8,128)(2,1)} %get-tuple-element.5), channel_id=1, source_target_pairs={{0,1},{1,2},{2,3},{4,5},{5,6},{6,7},{8,9},{9,10},{10,11},{12,13},{... | collective-permute-start | bytes 1253384 | tf_op jit(solution)/shard_map/ppermute | solution.py:15
  187.1 11.6 %copy-start.6 = (bf16[16,16,16,4]{3,2,1,0:T(8,128)(2,1)S(1)}, bf16[16,16,16,4]{3,2,1,0:T(8,128)(2,1)}, u32[]{:S(2)}) copy-start(bf16[16,16,16,4]{3,2,1,0:T(8,128)(2,1)} %copy.36) | copy-start | bytes 98308
  187.1 11.6 %copy-start.8 = (bf16[16,16,16,4]{3,2,1,0:T(8,128)(2,1)S(1)}, bf16[16,16,16,4]{3,2,1,0:T(8,128)(2,1)}, u32[]{:S(2)}) copy-start(bf16[16,16,16,4]{3,2,1,0:T(8,128)(2,1)} %copy.35) | copy-start | bytes 98308
  (7 other events, 55.7 us)
where the time goes:
time: 232 us; the launch traced here: 230 us
  local copies, waits for them, and re-layouts  79.1 us (34%)
  other arithmetic  64.9 us (28%)
  starting transfers between devices  57.6 us (25%)
  matrix products  26.6 us (11%)
    ppermute x6, starting transfers between devices, padded_2(): lax.ppermute(tail, axis, [(i, (i + 1) % count) for i in range(ends)])  25.7 us
    dot_general x2, matrix products, conv_padded(): lax.dot_general(padded, band, (((along,), (0,)), ((), ())), precision=lax...  23 us
    add x2, other arithmetic, conv_padded(): total + kernel_row[offset] * lax.slice_in_dim(padded, offset, offset + le...  22.7 us
    all_to_all x3, starting transfers between devices, copy_for_each(): lax.all_to_all(jnp.broadcast_to(shard[None], (devices, *shard.shape)), ax...  20.3 us
    reduce_sum x2, other arithmetic, restrict(): return shaped.mean(axis=(2, 4, 6))  15.3 us
    unnamed x40, local copies, waits for them, and re-layouts  14.3 us
    reshape x2, local copies, waits for them, and re-layouts, prolong(): return jnp.repeat(values, factor, axis=3)  13.2 us
    ppermute x6, starting transfers between devices, padded_2(): lax.ppermute(head, axis, [((i + 1) % count, i) for i in range(ends)])  11.6 us
  transfers between devices with their start and end apart: 15, of which 2 were waited for; matrix products, arithmetic and copies ran while one was open for 47% of the time, Pallas kernels for 0%

commit v1 on v0

v1 whole, which is shorter than its diff:
```python
import functools

import jax
import jax.numpy as jnp
from jax import lax
from jax.experimental import pallas as pl
from jax.experimental.pallas import tpu as pltpu
from jax.sharding import PartitionSpec as P

F32 = jnp.float32
BF16 = jnp.bfloat16
MESH = pl.DeviceIdType.MESH
NGX, NGY, NGZ = 4, 16, 4
NCH = 2
VCH = 16 // NCH
PCH = 8 // NCH
SIDES = [(1, 0), (-1, 0), (0, 1), (0, -1), (1, 1), (1, -1), (-1, 1), (-1, -1)]


def iota(shape, dim):
    return lax.broadcasted_iota(jnp.int32, shape, dim)


def nn(a, b):
    return lax.dot_general(a, b, (((1,), (0,)), ((), ())), preferred_element_type=F32)


def nt(a, b):
    return lax.dot_general(a, b, (((1,), (1,)), ((), ())), preferred_element_type=F32)


def tn(a, b):
    return lax.dot_general(a, b, (((0,), (0,)), ((), ())), preferred_element_type=F32)


def hi_lo(w):
    hi = w.astype(BF16)
    return hi, (w - hi.astype(F32)).astype(BF16)


def taps_at(taps_ref, row, offset):
    value = jnp.zeros(offset.shape, F32)
    for k in range(9):
        value = jnp.where(offset == k, taps_ref[row, k], value)
    return value


def kernel(
    field, fine_taps, coarse_taps, top, out,
    fld, halo, strips, cl, ch, tt, edge_out, edge_in, base, res,
    wf, wc, xw, xh, gsel, rx, perm, kv, kp, gath, tile_in, psum, acc, prol,
    fs, fr, cs, cr, es, er, s1s, s1r, s2s, s2r, s3s, s3r, lsem, osem,
):
    gx, gy, gz = lax.axis_index("gx"), lax.axis_index("gy"), lax.axis_index("gz")

    def dev(dx, dy, dz):
        return (
            lax.rem(gx + (dx + NGX), NGX),
            lax.rem(gy + (dy + NGY), NGY),
            lax.rem(gz + (dz + NGZ), NGZ),
        )

    def remote(src, dst, ssem, rsem, to):
        return pltpu.make_async_remote_copy(
            src_ref=src, dst_ref=dst, send_sem=ssem, recv_sem=rsem, device_id=to, device_id_type=MESH
        )

    load_field = pltpu.make_async_copy(field, fld, lsem.at[0])
    load_top = pltpu.make_async_copy(top, kv, lsem.at[1])
    load_field.start()
    load_top.start()

    barrier = pltpu.get_barrier_semaphore()
    partners = [(i, 0, 0) for i in range(1, NGX)] + [(0, i, 0) for i in range(1, NGY)]
    partners += [(0, 0, i) for i in range(1, NGZ)] + [(0, dy, dz) for dz, dy in SIDES[4:]]
    for d in partners:
        pl.semaphore_signal(barrier, inc=1, device_id=dev(*d), device_id_type=MESH)

    r, c = iota((192, 256), 0), iota((192, 256), 1)
    z, y = c >> 4, c & 15
    strip_z, strip_y = (r & 63) >> 2, (r & 3) + jnp.where(r >= 64, 12, 0)
    q = r - 128
    cz, cy = ((q >> 5) << 2) + ((q >> 2) & 3), (((q >> 4) & 1) << 2) + (q & 3)
    is_strip = (z == strip_z) & (y == strip_y)
    is_mean = ((z >> 1) == cz) & ((y >> 1) == cy)
    gsel[...] = jnp.where(
        r < 128, jnp.where(is_strip, 1.0, 0.0), jnp.where(is_mean, 0.25, 0.0)
    ).astype(BF16)
    k, n = iota((512, 128), 0), iota((512, 128), 1)
    rx[...] = jnp.where(((k >> 8) == (n >> 6)) & (((k & 127) >> 1) == (n & 63)), 0.5, 0.0).astype(BF16)

    load_field.wait()
    r, c = iota((32, 256), 0), iota((32, 256), 1)
    rows = jnp.where(((r & 15) == (c >> 4)) & (((c & 15) >> 3) == (r >> 4)), 1.0, 0.0).astype(BF16)
    for zt in range(2):
        total = fld[:, pl.ds(zt * 128, 16), :].astype(F32)
        for i in range(1, 8):
            total = total + fld[:, pl.ds(zt * 128 + i * 16, 16), :].astype(F32)
        total = total.reshape(256, 128)
        hi, lo = hi_lo(total)
        lo2 = (total - hi.astype(F32) - lo.astype(F32)).astype(BF16)
        both = nn(rows, hi) + nn(rows, lo) + nn(rows, lo2)
        for yt in range(2):
            psum[:, pl.ds((zt * 2 + yt) * 128, 128)] = both[yt * 16 : yt * 16 + 16]
    k, n = iota((512, 128), 0), iota((512, 128), 1)
    spot = lax.rem(gz, 2) * 64 + ((k >> 7) << 4) + ((k & 127) >> 3)
    place = jnp.where(n == spot, 1.0 / 512.0, 0.0).astype(BF16)
    sums = psum[...]
    hi, lo = hi_lo(sums)
    lo2 = (sums - hi.astype(F32) - lo.astype(F32)).astype(BF16)
    tile_in[gz] = (nn(hi, place) + nn(lo, place) + nn(lo2, place)).astype(BF16)

    pl.semaphore_wait(barrier, len(partners))

    stage1 = []
    for d in range(1, NGZ):
        cp = remote(tile_in.at[gz], tile_in.at[gz], s1s.at[d - 1], s1r.at[d - 1], dev(0, 0, d))
        cp.start()
        stage1.append(cp)

    def fine_copy(h, i):
        dz, dy = SIDES[i]
        vs = pl.ds(h * VCH, VCH)
        if dy == 0:
            src = fld.at[vs, pl.ds(192 if dz > 0 else 0, 64)]
            dst = halo.at[vs, pl.ds(0 if dz > 0 else 64, 64)]
        elif dz == 0:
            src = strips.at[1 if dy > 0 else 0, vs]
            dst = halo.at[vs, pl.ds(128 if dy > 0 else 192, 64)]
        else:
            src = strips.at[1 if dy > 0 else 0, vs, pl.ds(48 if dz > 0 else 0, 16)]
            dst = halo.at[vs, pl.ds(256 + (0 if dz > 0 else 32) + (0 if dy > 0 else 16), 16)]
        return remote(src, dst, fs.at[h, i], fr.at[h, i], dev(0, dy, dz))

    def coarse_copy(i):
        dz, dy = SIDES[i]
        if dy == 0:
            src, dst = cl.at[:, 1 if dz > 0 else 0], ch.at[:, pl.ds(0 if dz > 0 else 2, 2)]
        elif dz == 0:
            src, dst = cl.at[:, :, 1 if dy > 0 else 0], ch.at[:, pl.ds(4 if dy > 0 else 6, 2)]
        else:
            src = cl.at[:, 1 if dz > 0 else 0, 1 if dy > 0 else 0]
            dst = ch.at[:, 8 + (0 if dz > 0 else 2) + (0 if dy > 0 else 1)]
        return remote(src, dst, cs.at[i], cr.at[i], dev(0, dy, dz))

    fine = [[fine_copy(h, i) for i in range(8)] for h in range(NCH)]
    coarse = [coarse_copy(i) for i in range(8)]
    for h in range(NCH):
        fine[h][0].start()
        fine[h][1].start()

    def cut(p, carry):
        pair = jnp.concatenate([fld[2 * p], fld[2 * p + 1]], axis=1)
        got = nn(gsel[...], pair)
        for v in range(2):
            for side in range(2):
                strips[side, 2 * p + v] = got[side * 64 : side * 64 + 64, v * 128 : v * 128 + 128].astype(BF16)
        means = got[128:192]
        hi, lo = hi_lo(means)
        both = jnp.concatenate([hi[:, :128], lo[:, :128], hi[:, 128:], lo[:, 128:]], axis=1)
        cl[p] = nn(both, rx[...]).astype(BF16).reshape(2, 2, 16, 128)
        return carry

    lax.fori_loop(0, 8, cut, 0)
    for i in range(2, 8):
        fine[0][i].start()
    for i in range(8):
        coarse[i].start()
    for h in range(1, NCH):
        for i in range(2, 8):
            fine[h][i].start()

    for cp in stage1:
        cp.wait()
    for half in range(2):
        gath[gx, gy, half] = tile_in[2 * half] + tile_in[2 * half + 1]
    stage2 = []
    for d in range(1, NGY):
        cp = remote(gath.at[gx, gy], gath.at[gx, gy], s2s.at[d - 1], s2r.at[d - 1], dev(0, d, 0))
        cp.start()
        stage2.append(cp)

    zmin, zmax = jnp.where(gz > 0, -99, 0), jnp.where(gz < NGZ - 1, 99, 0)
    ymin, ymax = jnp.where(gy > 0, -99, 0), jnp.where(gy < NGY - 1, 99, 0)

    def zy_weights(taps_ref, zi, yi, zo, yo, side):
        ok = (zi >= zmin) & (yi >= ymin) & (zi < zmax + side) & (yi < ymax + side)
        w = taps_at(taps_ref, 0, zi - zo + 4) * taps_at(taps_ref, 1, yi - yo + 4)
        return hi_lo(jnp.where(ok, w, 0.0))

    o, c = iota((256, 256), 0), iota((256, 256), 1)
    hi, lo = zy_weights(fine_taps, c >> 4, c & 15, o >> 4, o & 15, 16)
    wf[0, :, pl.ds(0, 256)] = hi
    wf[1, :, pl.ds(0, 256)] = lo
    o, c = iota((256, 320), 0), iota((256, 320), 1)
    z4, y4, q = (c >> 2) & 3, c & 3, (c >> 4) & 3
    zi = jnp.where(
        c < 64, (c >> 4) - 4, jnp.where(c < 128, (c >> 4) + 12, jnp.where(c < 256, (c & 63) >> 2, jnp.where(q < 2, z4 - 4, z4 + 16)))
    )
    yi = jnp.where(
        c < 128, c & 15, jnp.where(c < 192, y4 - 4, jnp.where(c < 256, y4 + 16, jnp.where((q & 1) == 0, y4 - 4, y4 + 16)))
    )
    hi, lo = zy_weights(fine_taps, zi, yi, o >> 4, o & 15, 16)
    wf[0, :, pl.ds(256, 320)] = hi
    wf[1, :, pl.ds(256, 320)] = lo
    o, c = iota((256, 256), 0), iota((256, 256), 1)
    z4, y4, q = (c >> 2) & 3, c & 3, c >> 4
    first = (q & 1) * 4
    zi = jnp.where(
        q < 4, ((q >> 1) << 2) + z4,
        jnp.where(q < 6, z4 - 4, jnp.where(q < 8, z4 + 8, jnp.where(q < 12, first + z4, jnp.where(q < 14, z4 - 4, z4 + 8)))),
    )
    yi = jnp.where(
        q < 8, first + y4,
        jnp.where(q < 10, y4 - 4, jnp.where(q < 12, y4 + 8, jnp.where((q & 1) == 0, y4 - 4, y4 + 8))),
    )
    hi, lo = zy_weights(coarse_taps, zi, yi, o >> 5, (o & 15) >> 1, 8)
    wc[0] = hi
    wc[1] = lo

    k, n = iota((384, 256), 0), iota((384, 256), 1)
    xo, v = n & 127, n >> 7
    w = jnp.where(
        k < 256,
        jnp.where((k >> 7) == v, taps_at(fine_taps, 2, (k & 127) - xo + 4), 0.0),
        jnp.where(((k >> 6) & 1) == v, taps_at(coarse_taps, 2, (k & 63) - (xo >> 1) + 4), 0.0),
    )
    hi, lo = hi_lo(w)
    xw[0] = hi
    xw[1] = lo
    r, n = iota((32, 256), 0), iota((32, 256), 1)
    xo, v, e = n & 127, n >> 7, r & 3
    right = r >= 16
    w = jnp.where(
        (r & 8) == 0,
        taps_at(fine_taps, 2, e + jnp.where(right, 128, -4) - xo + 4),
        taps_at(coarse_taps, 2, e + jnp.where(right, 64, -4) - (xo >> 1) + 4),
    )
    there = jnp.where(right, jnp.where(gx < NGX - 1, 1, 0), jnp.where(gx > 0, 1, 0)) == 1
    hi, lo = hi_lo(jnp.where(there & (((r >> 2) & 1) == v), w, 0.0))
    xh[pl.ds(0, 32)] = hi
    xh[pl.ds(32, 32)] = lo

    for cp in stage2:
        cp.wait()
    stage3 = []
    for d in range(1, NGX):
        cp = remote(gath.at[gx], gath.at[gx], s3s.at[d - 1], s3r.at[d - 1], dev(d, 0, 0))
        cp.start()
        stage3.append(cp)

    load_top.wait()
    k, n = iota((512, 512), 0), iota((512, 512), 1)
    target = (((k >> 4) & 3) << 7) + ((k >> 7) << 5) + (((k >> 6) & 1) << 4) + (k & 15)
    perm[...] = jnp.where(n == target, 1.0, 0.0).astype(BF16)

    def reorder(g, carry):
        parts = []
        for half in range(2):
            pieces = [
                kv[:, pl.ds(pl.multiple_of(((half * 4 + z4) * 16 + g) * 128, 128), 128)] for z4 in range(4)
            ]
            parts.append(jnp.concatenate(pieces, axis=1))
        got = nn(jnp.concatenate(parts, axis=0), perm[...]).astype(BF16)
        for half in range(2):
            for x in range(4):
                kp[x, g, :, pl.ds(half * 128, 128)] = got[half * 64 : half * 64 + 64, x * 128 : x * 128 + 128]
        return carry

    lax.fori_loop(0, NGY, reorder, 0)

    r, c = iota((32, 384), 0), iota((32, 384), 1)
    t, e, right = (r >> 2) & 3, r & 3, r >= 16
    spot = jnp.where(
        t < 2, t * 128 + jnp.where(right, 124, 0), 256 + (t & 1) * 64 + jnp.where(right, 60, 0)
    )
    pick = jnp.where(c == spot + e, 1.0, 0.0).astype(BF16)

    def zy_pass(p, carry):
        pair = jnp.concatenate([fld[2 * p], fld[2 * p + 1]], axis=1)
        near = jnp.concatenate([halo[2 * p], halo[2 * p + 1]], axis=1)
        got = (
            nn(wf[0, :, pl.ds(0, 256)], pair) + nn(wf[0, :, pl.ds(256, 320)], near)
            + nn(wf[1, :, pl.ds(0, 256)], pair) + nn(wf[1, :, pl.ds(256, 320)], near)
        )
        cells = jnp.concatenate([cl[p].reshape(64, 128), ch[p].reshape(192, 128)], axis=0)
        got_coarse = nn(wc[0], cells) + nn(wc[1], cells)
        both = jnp.concatenate([got.astype(BF16), got_coarse.astype(BF16)], axis=1)
        tt[p] = both
        ends = nt(pick, both).astype(BF16)
        edge_out[0, p] = ends[:16]
        edge_out[1, p] = ends[16:]
        return carry

    edges = []
    for cp in coarse:
        cp.wait()
    for h in range(NCH):
        for cp in fine[h]:
            cp.wait()
        lax.fori_loop(h * PCH, (h + 1) * PCH, zy_pass, 0)
        ps = pl.ds(h * PCH, PCH)
        left = remote(edge_out.at[0, ps], edge_in.at[1, ps], es.at[h, 0], er.at[h, 0], dev(-1, 0, 0))
        right = remote(edge_out.at[1, ps], edge_in.at[0, ps], es.at[h, 1], er.at[h, 1], dev(1, 0, 0))
        left.start()
        right.start()
        edges.append((left, right))

    def x_pass(p, carry):
        both = tt[p]
        ends = jnp.concatenate([edge_in[0, p], edge_in[1, p]], axis=0)
        base[p] = nn(both, xw[0]) + nn(both, xw[1]) + tn(jnp.concatenate([ends, ends], axis=0), xh[...])
        return carry

    for h in range(NCH):
        for cp in edges[h]:
            cp.wait()
        lax.fori_loop(h * PCH, (h + 1) * PCH, x_pass, 0)

    def gather_dot(x):
        def add(g, total):
            block = jnp.concatenate([gath[x, g, 0], gath[x, g, 1]], axis=1)
            return total + nt(kp[x, g], block)

        acc[...] = acc[...] + lax.fori_loop(0, NGY, add, jnp.zeros((64, 16), F32))

    acc[...] = jnp.zeros((64, 16), F32)
    gather_dot(gx)
    for d in range(1, NGX):
        stage3[d - 1].wait()
        gather_dot(lax.rem(gx + (NGX - d), NGX))

    k, n = iota((64, 512), 0), iota((64, 512), 1)
    spread = jnp.where(k == ((n >> 7) << 4) + ((n & 127) >> 3), 1.0, 0.0).astype(BF16)
    sums = acc[...]
    hi, lo = hi_lo(sums)
    lo2 = (sums - hi.astype(F32) - lo.astype(F32)).astype(BF16)
    prol[...] = tn(hi, spread) + tn(lo, spread) + tn(lo2, spread)

    for p in range(8):
        for v in range(2):
            for zt in range(2):
                for yt in range(2):
                    row = prol[pl.ds(2 * p + v, 1), pl.ds((zt * 2 + yt) * 128, 128)]
                    block = jnp.broadcast_to(row, (8, 128))
                    for i in range(8):
                        rows = pl.ds((zt * 8 + i) * 16 + yt * 8, 8)
                        base[p, rows, pl.ds(v * 128, 128)] = base[p, rows, pl.ds(v * 128, 128)] + block

    def finish(p, carry):
        for v in range(2):
            res[2 * p + v] = base[p, :, pl.ds(v * 128, 128)].astype(BF16)
        return carry

    lax.fori_loop(0, 8, finish, 0)
    store = pltpu.make_async_copy(res, out, osem.at[0])
    store.start()
    store.wait()


def shards(field, fine_taps, coarse_taps, top_kernel):
    vm = pltpu.VMEM
    dma = pltpu.SemaphoreType.DMA
    smem = pl.BlockSpec(memory_space=pltpu.SMEM)
    hbm = pl.BlockSpec(memory_space=pl.ANY)
    out = pl.pallas_call(
        kernel,
        name="covariance",
        out_shape=jax.ShapeDtypeStruct((16, 256, 128), BF16),
        in_specs=[hbm, smem, smem, hbm],
        out_specs=hbm,
        scratch_shapes=[
            vm((16, 256, 128), BF16),
            vm((16, 320, 128), BF16),
            vm((2, 16, 64, 128), BF16),
            vm((8, 2, 2, 16, 128), BF16),
            vm((8, 12, 16, 128), BF16),
            vm((8, 256, 384), BF16),
            vm((2, 8, 16, 256), BF16),
            vm((2, 8, 16, 256), BF16),
            vm((8, 256, 256), F32),
            vm((16, 256, 128), BF16),
            vm((2, 256, 576), BF16),
            vm((2, 256, 256), BF16),
            vm((2, 384, 256), BF16),
            vm((64, 256), BF16),
            vm((192, 256), BF16),
            vm((512, 128), BF16),
            vm((512, 512), BF16),
            vm((64, 16384), BF16),
            vm((4, 16, 64, 256), BF16),
            vm((4, 16, 2, 16, 128), BF16),
            vm((4, 16, 128), BF16),
            vm((16, 512), F32),
            vm((64, 16), F32),
            vm((16, 512), F32),
            dma((NCH, 8)), dma((NCH, 8)),
            dma((8,)), dma((8,)),
            dma((NCH, 2)), dma((NCH, 2)),
            dma((3,)), dma((3,)),
            dma((15,)), dma((15,)),
            dma((3,)), dma((3,)),
            dma((2,)), dma((1,)),
        ],
        compiler_params=pltpu.CompilerParams(
            collective_id=1, has_side_effects=True, vmem_limit_bytes=40 << 20
        ),
    )(field.reshape(16, 256, 128), fine_taps, coarse_taps, top_kernel.reshape(64, 16384))
    return out.reshape(field.shape)


def solution(mesh):
    return jax.shard_map(
        shards,
        mesh=mesh,
        in_specs=(P(None, "gz", "gy", "gx"), P(), P(), P("gz", "gy", "gx", None)),
        out_specs=P(None, "gz", "gy", "gx"),
        check_vma=False,
    )
```

time: 232 us -> 53 us (0.23)
  local copies, waits for them, and re-layouts: 79.1 us -> 5.15 us
  other arithmetic: 64.9 us -> 0 us
  starting transfers between devices: 57.6 us -> 0 us
  Pallas kernels: 0 us -> 47.7 us
  matrix products: 26.6 us -> 0 us
    pallas_call x0 -> x1, Pallas kernels: none -> 47.7 us  [shards(): pl.pallas_call(kernel, name='covariance', out_shape=jax.ShapeDtypeStruct(...]
    ppermute x12 -> x0, starting transfers between devices: 37.3 us -> none  [the longest x6 25.7 us: padded_2(): lax.ppermute(tail, axis, [(i, (i + 1) % count) for i in range(ends)])]
    add x3 -> x0, other arithmetic: 29.5 us -> none  [the longest x2 22.7 us: conv_padded(): total + kernel_row[offset] * lax.slice_in_dim(padded, offset, offset + le...]
    reshape x4 -> x0, local copies, waits for them, and re-layouts: 28.6 us -> none  [the longest x2 13.2 us: prolong(): return jnp.repeat(values, factor, axis=3)]
    dot_general x3 -> x0, matrix products: 26.6 us -> none  [the longest x2 23 us: conv_padded(): lax.dot_general(padded, band, (((along,), (0,)), ((), ())), precision=lax...]
    all_to_all x3 -> x0, starting transfers between devices: 20.3 us -> none  [copy_for_each(): lax.all_to_all(jnp.broadcast_to(shard[None], (devices, *shard.shape)), ax...]
    reduce_sum x2 -> x0, other arithmetic: 15.3 us -> none  [restrict(): return shaped.mean(axis=(2, 4, 6))]
    broadcast_in_dim x12 -> x0, local copies, waits for them, and re-layouts: 12.9 us -> none  [the longest x2 10.8 us: prolong(): return jnp.repeat(values, factor, axis=3)]
  transfers between devices with their start and end apart: 15 -> 0, of which waited for: 2 -> 0; matrix products, arithmetic and copies ran while one was open for 47% -> 0% of each run, Pallas kernels for 0% -> 0%
where the time goes in v1:
time: 53 us; the launch traced here: 52.9 us
  Pallas kernels  47.7 us (90%)
  local copies, waits for them, and re-layouts  5.15 us (10%)
    pallas_call x1, Pallas kernels, shards(): pl.pallas_call(kernel, name='covariance', out_shape=jax.ShapeDtypeStruct(...  47.7 us
    unnamed x9, local copies, waits for them, and re-layouts  5.15 us

profile of v1, /device:TPU:1, one launch (start us, length us, event | category | flops | bytes accessed | tf_op | source)
XLA Modules:
  0.0 52.9 jit_solution(2485461705152843679)
XLA Ops:
  0.0 0.0 copy-start
  0.0 1.6 %copy-done = bf16[2,2,16,16384]{3,2,1,0:T(8,128)(2,1)S(1)} copy-done((bf16[2,2,16,16384]{3,2,1,0:T(8,128)(2,1)S(1)}, bf16[2,2,16,16384]{3,2,1,0:T(8,128)(2,1)}, u32[]{:S(2)}) %copy-start) | copy-done | bytes 2097176
  1.6 0.0 copy-start.1
  1.6 1.2 %copy-done.1 = bf16[16,16,16,128]{3,2,1,0:T(8,128)(2,1)S(1)} copy-done((bf16[16,16,16,128]{3,2,1,0:T(8,128)(2,1)S(1)}, bf16[16,16,16,128]{3,2,1,0:T(8,128)(2,1)}, u32[]{:S(2)}) %copy-start.1) | copy-done | bytes 1048600
  2.8 0.0 copy-start.2
  2.8 0.7 %copy-done.2 = f32[3,9]{1,0:T(4,128)S(1)} copy-done((f32[3,9]{1,0:T(4,128)S(1)}, f32[3,9]{1,0:T(4,128)}, u32[]{:S(2)}) %copy-start.2) | copy-done | bytes 132
  3.5 0.0 copy-start.3
  3.5 0.7 %copy-done.3 = f32[3,9]{1,0:T(4,128)S(1)} copy-done((f32[3,9]{1,0:T(4,128)S(1)}, f32[3,9]{1,0:T(4,128)}, u32[]{:S(2)}) %copy-start.3) | copy-done | bytes 132
  4.2 47.7 %covariance.1 = bf16[16,256,128]{2,1,0:T(8,128)(2,1)S(1)} custom-call(bf16[16,256,128]{2,1,0:T(8,128)(2,1)S(1)} %bitcast.5, f32[3,9]{1,0:T(4,128)S(1)} %copy-done.2, f32[3,9]{1,0:T(4,128)S(1)} %copy-done.3, bf16[64,16384]{1,0:T(8,128)(2,1)S(1)} %bitcast.4), custom_call_target="tpu_custom_call" | custom-call | tf_op jit(solution)/shard_map/covariance/pallas_call | solution.py:366
  51.9 1.0 %copy.6 = bf16[16,16,16,128]{3,2,1,0:T(8,128)(2,1)} copy(bf16[16,16,16,128]{3,2,1,0:T(8,128)(2,1)S(1)} %bitcast.3) | data formatting | bytes 2097152
Async XLA Ops:
  0.0 1.6 %copy-start = (bf16[2,2,16,16384]{3,2,1,0:T(8,128)(2,1)S(1)}, bf16[2,2,16,16384]{3,2,1,0:T(8,128)(2,1)}, u32[]{:S(2)}) copy-start(bf16[2,2,16,16384]{3,2,1,0:T(8,128)(2,1)} %param.7) | copy-start | bytes 6291460
  1.6 1.2 %copy-start.1 = (bf16[16,16,16,128]{3,2,1,0:T(8,128)(2,1)S(1)}, bf16[16,16,16,128]{3,2,1,0:T(8,128)(2,1)}, u32[]{:S(2)}) copy-start(bf16[16,16,16,128]{3,2,1,0:T(8,128)(2,1)} %param.4) | copy-start | bytes 3145732
  2.8 0.7 %copy-start.2 = (f32[3,9]{1,0:T(4,128)S(1)}, f32[3,9]{1,0:T(4,128)}, u32[]{:S(2)}) copy-start(f32[3,9]{1,0:T(4,128)} %fine_taps.1) | copy-start | bytes 328
  3.5 0.7 %copy-start.3 = (f32[3,9]{1,0:T(4,128)S(1)}, f32[3,9]{1,0:T(4,128)}, u32[]{:S(2)}) copy-start(f32[3,9]{1,0:T(4,128)} %coarse_taps.1) | copy-start | bytes 328

commit v2 on v1

--- a/solution.py
+++ b/solution.py
@@ -46,7 +46,8 @@
 
 
 def kernel(
-    field, fine_taps, coarse_taps, top, out,
+    field, fine_hbm, coarse_hbm, top, out,
+    fine_taps, coarse_taps,
     fld, halo, strips, cl, ch, tt, edge_out, edge_in, base, res,
     wf, wc, xw, xh, gsel, rx, perm, kv, kp, gath, tile_in, psum, acc, prol,
     fs, fr, cs, cr, es, er, s1s, s1r, s2s, s2r, s3s, s3r, lsem, osem,
@@ -67,7 +68,11 @@
 
     load_field = pltpu.make_async_copy(field, fld, lsem.at[0])
     load_top = pltpu.make_async_copy(top, kv, lsem.at[1])
+    load_fine = pltpu.make_async_copy(fine_hbm, fine_taps, lsem.at[2])
+    load_coarse = pltpu.make_async_copy(coarse_hbm, coarse_taps, lsem.at[3])
     load_field.start()
+    load_fine.start()
+    load_coarse.start()
     load_top.start()
 
     barrier = pltpu.get_barrier_semaphore()
@@ -180,6 +185,8 @@
         cp.start()
         stage2.append(cp)
 
+    load_fine.wait()
+    load_coarse.wait()
     zmin, zmax = jnp.where(gz > 0, -99, 0), jnp.where(gz < NGZ - 1, 99, 0)
     ymin, ymax = jnp.where(gy > 0, -99, 0), jnp.where(gy < NGY - 1, 99, 0)
 
@@ -361,15 +368,16 @@
 def shards(field, fine_taps, coarse_taps, top_kernel):
     vm = pltpu.VMEM
     dma = pltpu.SemaphoreType.DMA
-    smem = pl.BlockSpec(memory_space=pltpu.SMEM)
-    hbm = pl.BlockSpec(memory_space=pl.ANY)
+    hbm = pl.BlockSpec(memory_space=pltpu.HBM)
     out = pl.pallas_call(
         kernel,
         name="covariance",
         out_shape=jax.ShapeDtypeStruct((16, 256, 128), BF16),
-        in_specs=[hbm, smem, smem, hbm],
+        in_specs=[hbm, hbm, hbm, hbm],
         out_specs=hbm,
         scratch_shapes=[
+            pltpu.SMEM((3, 9), F32),
+            pltpu.SMEM((3, 9), F32),
             vm((16, 256, 128), BF16),
             vm((16, 320, 128), BF16),
             vm((2, 16, 64, 128), BF16),
@@ -400,10 +408,10 @@
             dma((3,)), dma((3,)),
             dma((15,)), dma((15,)),
             dma((3,)), dma((3,)),
-            dma((2,)), dma((1,)),
+            dma((4,)), dma((1,)),
         ],
         compiler_params=pltpu.CompilerParams(
-            collective_id=1, has_side_effects=True, vmem_limit_bytes=40 << 20
+            collective_id=1, has_side_effects=True, vmem_limit_bytes=60 << 20
         ),
     )(field.reshape(16, 256, 128), fine_taps, coarse_taps, top_kernel.reshape(64, 16384))
     return out.reshape(field.shape)

time: 53 us -> 50.3 us (0.949)
  local copies, waits for them, and re-layouts: 5.15 us -> 2.42 us
    unnamed x9 -> x1, local copies, waits for them, and re-layouts: 5.15 us -> 2.42 us
where the time goes in v2:
time: 50.3 us; the launch traced here: 50.2 us
  Pallas kernels  47.8 us (95%)
  local copies, waits for them, and re-layouts  2.42 us (5%)
    pallas_call x1, Pallas kernels, shards(): pl.pallas_call(kernel, name='covariance', out_shape=jax.ShapeDtypeStruct(...  47.8 us
    unnamed x1, local copies, waits for them, and re-layouts  2.42 us

profile of v2, /device:TPU:1, one launch (start us, length us, event | category | flops | bytes accessed | tf_op | source)
XLA Modules:
  0.0 50.2 jit_solution(8121238612762541540)
XLA Ops:
  0.0 47.8 %covariance.1 = bf16[16,256,128]{2,1,0:T(8,128)(2,1)} custom-call(bf16[16,256,128]{2,1,0:T(8,128)(2,1)} %bitcast.5, f32[3,9]{1,0:T(4,128)} %fine_hbm.1, f32[3,9]{1,0:T(4,128)} %coarse_hbm.1, bf16[64,16384]{1,0:T(8,128)(2,1)} %bitcast.4), custom_call_target="tpu_custom_call" | custom-call | tf_op jit(solution)/shard_map/covariance/pallas_call | solution.py:372
  47.8 2.4 %copy.6 = bf16[16,16,16,128]{3,2,1,0:T(8,128)(2,1)} copy(bf16[16,16,16,128]{3,2,1,0:T(8,128)(2,1)} %bitcast.3) | data formatting | bytes 2097152

commit v3 on v2

--- a/solution.py
+++ b/solution.py
@@ -49,7 +49,7 @@
     field, fine_hbm, coarse_hbm, top, out,
     fine_taps, coarse_taps,
     fld, halo, strips, cl, ch, tt, edge_out, edge_in, base, res,
-    wf, wc, xw, xh, gsel, rx, perm, kv, kp, gath, tile_in, psum, acc, prol,
+    wf, wc, xw, xh, gsel, rx, perm, kv, kp, gath, tile_in, psum, prol,
     fs, fr, cs, cr, es, er, s1s, s1r, s2s, s2r, s3s, s3r, lsem, osem,
 ):
     gx, gy, gz = lax.axis_index("gx"), lax.axis_index("gy"), lax.axis_index("gz")
@@ -166,7 +166,7 @@
         cl[p] = nn(both, rx[...]).astype(BF16).reshape(2, 2, 16, 128)
         return carry
 
-    lax.fori_loop(0, 8, cut, 0)
+    lax.fori_loop(0, 8, cut, 0, unroll=4)
     for i in range(2, 8):
         fine[0][i].start()
     for i in range(8):
@@ -261,20 +261,23 @@
     target = (((k >> 4) & 3) << 7) + ((k >> 7) << 5) + (((k >> 6) & 1) << 4) + (k & 15)
     perm[...] = jnp.where(n == target, 1.0, 0.0).astype(BF16)
 
-    def reorder(g, carry):
+    def reorder(i, carry):
         parts = []
-        for half in range(2):
-            pieces = [
-                kv[:, pl.ds(pl.multiple_of(((half * 4 + z4) * 16 + g) * 128, 128), 128)] for z4 in range(4)
-            ]
-            parts.append(jnp.concatenate(pieces, axis=1))
+        for g in range(4):
+            for half in range(2):
+                pieces = [
+                    kv[:, pl.ds(pl.multiple_of(((half * 4 + z4) * 16 + i * 4 + g) * 128, 128), 128)]
+                    for z4 in range(4)
+                ]
+                parts.append(jnp.concatenate(pieces, axis=1))
         got = nn(jnp.concatenate(parts, axis=0), perm[...]).astype(BF16)
-        for half in range(2):
+        for g in range(8):
+            at = pl.ds(pl.multiple_of((i * 8 + g) * 128, 128), 128)
             for x in range(4):
-                kp[x, g, :, pl.ds(half * 128, 128)] = got[half * 64 : half * 64 + 64, x * 128 : x * 128 + 128]
+                kp[x, :, at] = got[g * 64 : g * 64 + 64, x * 128 : x * 128 + 128]
         return carry
 
-    lax.fori_loop(0, NGY, reorder, 0)
+    lax.fori_loop(0, 4, reorder, 0)
 
     r, c = iota((32, 384), 0), iota((32, 384), 1)
     t, e, right = (r >> 2) & 3, r & 3, r >= 16
@@ -305,7 +308,7 @@
     for h in range(NCH):
         for cp in fine[h]:
             cp.wait()
-        lax.fori_loop(h * PCH, (h + 1) * PCH, zy_pass, 0)
+        lax.fori_loop(h * PCH, (h + 1) * PCH, zy_pass, 0, unroll=2)
         ps = pl.ds(h * PCH, PCH)
         left = remote(edge_out.at[0, ps], edge_in.at[1, ps], es.at[h, 0], er.at[h, 0], dev(-1, 0, 0))
         right = remote(edge_out.at[1, ps], edge_in.at[0, ps], es.at[h, 1], er.at[h, 1], dev(1, 0, 0))
@@ -322,47 +325,43 @@
     for h in range(NCH):
         for cp in edges[h]:
             cp.wait()
-        lax.fori_loop(h * PCH, (h + 1) * PCH, x_pass, 0)
+        lax.fori_loop(h * PCH, (h + 1) * PCH, x_pass, 0, unroll=2)
 
     def gather_dot(x):
-        def add(g, total):
-            block = jnp.concatenate([gath[x, g, 0], gath[x, g, 1]], axis=1)
-            return total + nt(kp[x, g], block)
-
-        acc[...] = acc[...] + lax.fori_loop(0, NGY, add, jnp.zeros((64, 16), F32))
-
-    acc[...] = jnp.zeros((64, 16), F32)
-    gather_dot(gx)
+        tiles = [gath[x, g, half] for g in range(NGY) for half in range(2)]
+        return nt(kp[x], jnp.concatenate(tiles, axis=1))
+
+    sums = gather_dot(gx)
     for d in range(1, NGX):
         stage3[d - 1].wait()
-        gather_dot(lax.rem(gx + (NGX - d), NGX))
+        sums = sums + gather_dot(lax.rem(gx + (NGX - d), NGX))
 
     k, n = iota((64, 512), 0), iota((64, 512), 1)
     spread = jnp.where(k == ((n >> 7) << 4) + ((n & 127) >> 3), 1.0, 0.0).astype(BF16)
-    sums = acc[...]
     hi, lo = hi_lo(sums)
     lo2 = (sums - hi.astype(F32) - lo.astype(F32)).astype(BF16)
     prol[...] = tn(hi, spread) + tn(lo, spread) + tn(lo2, spread)
 
-    for p in range(8):
+    def finish(p, carry):
         for v in range(2):
             for zt in range(2):
-                for yt in range(2):
-                    row = prol[pl.ds(2 * p + v, 1), pl.ds((zt * 2 + yt) * 128, 128)]
-                    block = jnp.broadcast_to(row, (8, 128))
-                    for i in range(8):
-                        rows = pl.ds((zt * 8 + i) * 16 + yt * 8, 8)
-                        base[p, rows, pl.ds(v * 128, 128)] = base[p, rows, pl.ds(v * 128, 128)] + block
-
-    def finish(p, carry):
-        for v in range(2):
-            res[2 * p + v] = base[p, :, pl.ds(v * 128, 128)].astype(BF16)
+                rows = [
+                    prol[pl.ds(2 * p + v, 1), pl.ds((zt * 2 + yt) * 128, 128)] for yt in range(2)
+                ]
+                block = jnp.concatenate([jnp.broadcast_to(row, (8, 128)) for row in rows], axis=0)
+                for i in range(8):
+                    at = pl.ds((zt * 8 + i) * 16, 16)
+                    res[2 * p + v, at] = (base[p, at, pl.ds(v * 128, 128)] + block).astype(BF16)
         return carry
 
-    lax.fori_loop(0, 8, finish, 0)
-    store = pltpu.make_async_copy(res, out, osem.at[0])
-    store.start()
-    store.wait()
+    stores = []
+    for h in range(4):
+        lax.fori_loop(h * 2, h * 2 + 2, finish, 0, unroll=True)
+        vs = pl.ds(h * 4, 4)
+        stores.append(pltpu.make_async_copy(res.at[vs], out.at[vs], osem.at[h]))
+        stores[h].start()
+    for cp in stores:
+        cp.wait()
 
 
 def shards(field, fine_taps, coarse_taps, top_kernel):
@@ -396,11 +395,10 @@
             vm((512, 128), BF16),
             vm((512, 512), BF16),
             vm((64, 16384), BF16),
-            vm((4, 16, 64, 256), BF16),
+            vm((4, 64, 4096), BF16),
             vm((4, 16, 2, 16, 128), BF16),
             vm((4, 16, 128), BF16),
             vm((16, 512), F32),
-            vm((64, 16), F32),
             vm((16, 512), F32),
             dma((NCH, 8)), dma((NCH, 8)),
             dma((8,)), dma((8,)),
@@ -408,7 +406,7 @@
             dma((3,)), dma((3,)),
             dma((15,)), dma((15,)),
             dma((3,)), dma((3,)),
-            dma((4,)), dma((1,)),
+            dma((4,)), dma((4,)),
         ],
         compiler_params=pltpu.CompilerParams(
             collective_id=1, has_side_effects=True, vmem_limit_bytes=60 << 20

time: 50.3 us -> 40.4 us (0.80)
  Pallas kernels: 47.8 us -> 37.9 us
    pallas_call x1, Pallas kernels: 47.8 us -> 37.9 us  [shards(): pl.pallas_call(kernel, name='covariance', out_shape=jax.ShapeDtypeStruct(...]
where the time goes in v3:
time: 40.4 us; the launch traced here: 40.3 us
  Pallas kernels  37.9 us (94%)
  local copies, waits for them, and re-layouts  2.42 us (6%)
    pallas_call x1, Pallas kernels, shards(): pl.pallas_call(kernel, name='covariance', out_shape=jax.ShapeDtypeStruct(...  37.9 us
    unnamed x1, local copies, waits for them, and re-layouts  2.42 us

profile of v3, /device:TPU:1, one launch (start us, length us, event | category | flops | bytes accessed | tf_op | source)
XLA Modules:
  0.0 40.3 jit_solution(8000181342448514851)
XLA Ops:
  0.0 37.9 %covariance.1 = bf16[16,256,128]{2,1,0:T(8,128)(2,1)} custom-call(bf16[16,256,128]{2,1,0:T(8,128)(2,1)} %bitcast.5, f32[3,9]{1,0:T(4,128)} %fine_hbm.1, f32[3,9]{1,0:T(4,128)} %coarse_hbm.1, bf16[64,16384]{1,0:T(8,128)(2,1)} %bitcast.4), custom_call_target="tpu_custom_call" | custom-call | tf_op jit(solution)/shard_map/covariance/pallas_call | solution.py:371
  37.9 2.4 %copy.6 = bf16[16,16,16,128]{3,2,1,0:T(8,128)(2,1)} copy(bf16[16,16,16,128]{3,2,1,0:T(8,128)(2,1)} %bitcast.3) | data formatting | bytes 2097152

commit v4 on v3

--- a/solution.py
+++ b/solution.py
@@ -48,9 +48,9 @@
 def kernel(
     field, fine_hbm, coarse_hbm, top, out,
     fine_taps, coarse_taps,
-    fld, halo, strips, cl, ch, tt, edge_out, edge_in, base, res,
+    fld, halo, strips, cl, ch, tt, edge_out, edge_in, base,
     wf, wc, xw, xh, gsel, rx, perm, kv, kp, gath, tile_in, psum, prol,
-    fs, fr, cs, cr, es, er, s1s, s1r, s2s, s2r, s3s, s3r, lsem, osem,
+    fs, fr, cs, cr, es, er, s1s, s1r, s2s, s2r, s3s, s3r, lsem,
 ):
     gx, gy, gz = lax.axis_index("gx"), lax.axis_index("gy"), lax.axis_index("gz")
 
@@ -351,29 +351,24 @@
                 block = jnp.concatenate([jnp.broadcast_to(row, (8, 128)) for row in rows], axis=0)
                 for i in range(8):
                     at = pl.ds((zt * 8 + i) * 16, 16)
-                    res[2 * p + v, at] = (base[p, at, pl.ds(v * 128, 128)] + block).astype(BF16)
+                    out[2 * p + v, at] = (base[p, at, pl.ds(v * 128, 128)] + block).astype(BF16)
         return carry
 
-    stores = []
-    for h in range(4):
-        lax.fori_loop(h * 2, h * 2 + 2, finish, 0, unroll=True)
-        vs = pl.ds(h * 4, 4)
-        stores.append(pltpu.make_async_copy(res.at[vs], out.at[vs], osem.at[h]))
-        stores[h].start()
-    for cp in stores:
-        cp.wait()
+    lax.fori_loop(0, 8, finish, 0, unroll=True)
 
 
 def shards(field, fine_taps, coarse_taps, top_kernel):
     vm = pltpu.VMEM
     dma = pltpu.SemaphoreType.DMA
     hbm = pl.BlockSpec(memory_space=pltpu.HBM)
+    operands = [field.reshape(16, 256, 128), fine_taps, coarse_taps, top_kernel.reshape(64, 16384)]
+    operands = [pltpu.with_memory_space_constraint(a, pltpu.HBM) for a in operands]
     out = pl.pallas_call(
         kernel,
         name="covariance",
-        out_shape=jax.ShapeDtypeStruct((16, 256, 128), BF16),
+        out_shape=pltpu.VMEM((16, 256, 128), BF16),
         in_specs=[hbm, hbm, hbm, hbm],
-        out_specs=hbm,
+        out_specs=pl.BlockSpec(memory_space=pltpu.VMEM),
         scratch_shapes=[
             pltpu.SMEM((3, 9), F32),
             pltpu.SMEM((3, 9), F32),
@@ -386,7 +381,6 @@
             vm((2, 8, 16, 256), BF16),
             vm((2, 8, 16, 256), BF16),
             vm((8, 256, 256), F32),
-            vm((16, 256, 128), BF16),
             vm((2, 256, 576), BF16),
             vm((2, 256, 256), BF16),
             vm((2, 384, 256), BF16),
@@ -406,12 +400,12 @@
             dma((3,)), dma((3,)),
             dma((15,)), dma((15,)),
             dma((3,)), dma((3,)),
-            dma((4,)), dma((4,)),
+            dma((4,)),
         ],
         compiler_params=pltpu.CompilerParams(
-            collective_id=1, has_side_effects=True, vmem_limit_bytes=60 << 20
+            collective_id=1, has_side_effects=True, vmem_limit_bytes=40 << 20
         ),
-    )(field.reshape(16, 256, 128), fine_taps, coarse_taps, top_kernel.reshape(64, 16384))
+    )(*operands)
     return out.reshape(field.shape)
 
 

time: 40.4 us -> 38 us (0.941)
  local copies, waits for them, and re-layouts: 2.42 us -> 0.97 us
  Pallas kernels: 37.9 us -> 36.9 us
    unnamed x1, local copies, waits for them, and re-layouts: 2.42 us -> 0.97 us
    pallas_call x1, Pallas kernels: 37.9 us -> 36.9 us  [shards(): pl.pallas_call(kernel, name='covariance', out_shape=pltpu.VMEM((16, 256,...]
where the time goes in v4:
time: 38 us; the launch traced here: 37.9 us
  Pallas kernels  36.9 us (97%)
  local copies, waits for them, and re-layouts  0.97 us (3%)
    pallas_call x1, Pallas kernels, shards(): pl.pallas_call(kernel, name='covariance', out_shape=pltpu.VMEM((16, 256,...  36.9 us
    unnamed x1, local copies, waits for them, and re-layouts  0.97 us

profile of v4, /device:TPU:1, one launch (start us, length us, event | category | flops | bytes accessed | tf_op | source)
XLA Modules:
  0.0 37.9 jit_solution(1156467948025399900)
XLA Ops:
  0.0 36.9 %covariance.1 = bf16[16,256,128]{2,1,0:T(8,128)(2,1)S(1)} custom-call(bf16[16,256,128]{2,1,0:T(8,128)(2,1)} %bitcast.5, f32[3,9]{1,0:T(4,128)} %fine_hbm.1, f32[3,9]{1,0:T(4,128)} %coarse_hbm.1, bf16[64,16384]{1,0:T(8,128)(2,1)} %bitcast.4), custom_call_target="tpu_custom_call" | custom-call | tf_op jit(solution)/shard_map/covariance/pallas_call | solution.py:366
  36.9 1.0 %copy.6 = bf16[16,16,16,128]{3,2,1,0:T(8,128)(2,1)} copy(bf16[16,16,16,128]{3,2,1,0:T(8,128)(2,1)S(1)} %bitcast.3) | data formatting | bytes 2097152

commit v5 on v4

--- a/solution.py
+++ b/solution.py
@@ -11,10 +11,9 @@
 BF16 = jnp.bfloat16
 MESH = pl.DeviceIdType.MESH
 NGX, NGY, NGZ = 4, 16, 4
-NCH = 2
+NCH = 4
 VCH = 16 // NCH
 PCH = 8 // NCH
-SIDES = [(1, 0), (-1, 0), (0, 1), (0, -1), (1, 1), (1, -1), (-1, 1), (-1, -1)]
 
 
 def iota(shape, dim):
@@ -48,7 +47,7 @@
 def kernel(
     field, fine_hbm, coarse_hbm, top, out,
     fine_taps, coarse_taps,
-    fld, halo, strips, cl, ch, tt, edge_out, edge_in, base,
+    fld, halo, strips, cl, ch, tt, edge_out, edge_in, relay,
     wf, wc, xw, xh, gsel, rx, perm, kv, kp, gath, tile_in, psum, prol,
     fs, fr, cs, cr, es, er, s1s, s1r, s2s, s2r, s3s, s3r, lsem,
 ):
@@ -77,7 +76,7 @@
 
     barrier = pltpu.get_barrier_semaphore()
     partners = [(i, 0, 0) for i in range(1, NGX)] + [(0, i, 0) for i in range(1, NGY)]
-    partners += [(0, 0, i) for i in range(1, NGZ)] + [(0, dy, dz) for dz, dy in SIDES[4:]]
+    partners += [(0, 0, i) for i in range(1, NGZ)]
     for d in partners:
         pl.semaphore_signal(barrier, inc=1, device_id=dev(*d), device_id_type=MESH)
 
@@ -91,8 +90,97 @@
     gsel[...] = jnp.where(
         r < 128, jnp.where(is_strip, 1.0, 0.0), jnp.where(is_mean, 0.25, 0.0)
     ).astype(BF16)
+    r, c = iota((64, 128), 0), iota((64, 128), 1)
+    spot = (((r >> 4) & 1) << 6) + (((r >> 2) & 3) << 4) + (r & 3) + jnp.where(r >= 32, 12, 0)
+    rsel = jnp.where(c == spot, 1.0, 0.0).astype(BF16)
     k, n = iota((512, 128), 0), iota((512, 128), 1)
     rx[...] = jnp.where(((k >> 8) == (n >> 6)) & (((k & 127) >> 1) == (n & 63)), 0.5, 0.0).astype(BF16)
+
+    load_fine.wait()
+    load_coarse.wait()
+    zmin, zmax = jnp.where(gz > 0, -99, 0), jnp.where(gz < NGZ - 1, 99, 0)
+    ymin, ymax = jnp.where(gy > 0, -99, 0), jnp.where(gy < NGY - 1, 99, 0)
+
+    def spread_taps(taps_ref, row, low, high, target, source):
+        r, k = iota((16, 32), 0), iota((16, 32), 1)
+        ok = (k - 4 >= low) & (k - 4 < high)
+        table = jnp.where(ok, taps_at(taps_ref, row, k - r), 0.0)
+        hi, lo = hi_lo(table)
+        lo2 = (table - hi.astype(F32) - lo.astype(F32)).astype(BF16)
+        k = iota((32, source.shape[1]), 0)
+        columns = jnp.where(k == source + 4, 1.0, 0.0).astype(BF16)
+        k = iota((256, 48), 1)
+        rows = jnp.where((k & 15) == target, 1.0, 0.0).astype(BF16)
+        return nn(rows, nn(jnp.concatenate([hi, lo, lo2], axis=0), columns).astype(BF16))
+
+    o = iota((256, 48), 0)
+    c = iota((32, 576), 1)
+    near = c - 256
+    z4, y4, q = (c >> 2) & 3, c & 3, (c >> 4) & 3
+    zi = jnp.where(
+        c < 256, c >> 4,
+        jnp.where(
+            near < 64, (near >> 4) - 4,
+            jnp.where(near < 128, (near >> 4) + 12, jnp.where(near < 256, (near & 63) >> 2, jnp.where((q & 1) == 0, z4 - 4, z4 + 16))),
+        ),
+    )
+    yi = jnp.where(
+        near < 128, c & 15,
+        jnp.where(near < 192, y4 - 4, jnp.where(near < 256, y4 + 16, jnp.where(q < 2, y4 - 4, y4 + 16))),
+    )
+    hi, lo = hi_lo(
+        spread_taps(fine_taps, 0, zmin, zmax + 16, o >> 4, zi)
+        * spread_taps(fine_taps, 1, ymin, ymax + 16, o & 15, yi)
+    )
+    wf[0] = hi
+    wf[1] = lo
+    c = iota((32, 256), 1)
+    z4, y4, q = (c >> 2) & 3, c & 3, c >> 4
+    first = (q & 1) * 4
+    zi = jnp.where(
+        q < 4, ((q >> 1) << 2) + z4,
+        jnp.where(q < 6, z4 - 4, jnp.where(q < 8, z4 + 8, jnp.where(q < 12, first + z4, jnp.where((q & 1) == 0, z4 - 4, z4 + 8)))),
+    )
+    yi = jnp.where(
+        q < 8, first + y4,
+        jnp.where(q < 10, y4 - 4, jnp.where(q < 12, y4 + 8, jnp.where(q < 14, y4 - 4, y4 + 8))),
+    )
+    hi, lo = hi_lo(
+        spread_taps(coarse_taps, 0, zmin, zmax + 8, o >> 5, zi)
+        * spread_taps(coarse_taps, 1, ymin, ymax + 8, (o & 15) >> 1, yi)
+    )
+    wc[0] = hi
+    wc[1] = lo
+
+    k, n = iota((128, 128), 0), iota((128, 128), 1)
+    fine_parts = hi_lo(taps_at(fine_taps, 2, k - n + 4))
+    k, n = iota((64, 128), 0), iota((64, 128), 1)
+    coarse_parts = hi_lo(taps_at(coarse_taps, 2, k - (n >> 1) + 4))
+    for part in range(2):
+        for v in range(2):
+            own, other = pl.ds(v * 128, 128), pl.ds(128 - v * 128, 128)
+            xw[part, pl.ds(v * 128, 128), own] = fine_parts[part]
+            xw[part, pl.ds(v * 128, 128), other] = jnp.zeros((128, 128), BF16)
+            xw[part, pl.ds(256 + v * 64, 64), own] = coarse_parts[part]
+            xw[part, pl.ds(256 + v * 64, 64), other] = jnp.zeros((64, 128), BF16)
+    r, n = iota((32, 256), 0), iota((32, 256), 1)
+    xo, v, e = n & 127, n >> 7, r & 3
+    right = r >= 16
+    w = jnp.where(
+        (r & 8) == 0,
+        taps_at(fine_taps, 2, e + jnp.where(right, 128, -4) - xo + 4),
+        taps_at(coarse_taps, 2, e + jnp.where(right, 64, -4) - (xo >> 1) + 4),
+    )
+    there = jnp.where(right, jnp.where(gx < NGX - 1, 1, 0), jnp.where(gx > 0, 1, 0)) == 1
+    hi, lo = hi_lo(jnp.where(there & (((r >> 2) & 1) == v), w, 0.0))
+    xh[pl.ds(0, 32)] = hi
+    xh[pl.ds(32, 32)] = lo
+    r, c = iota((32, 384), 0), iota((32, 384), 1)
+    t, e, right = (r >> 2) & 3, r & 3, r >= 16
+    spot = jnp.where(
+        t < 2, t * 128 + jnp.where(right, 124, 0), 256 + (t & 1) * 64 + jnp.where(right, 60, 0)
+    )
+    pick = jnp.where(c == spot + e, 1.0, 0.0).astype(BF16)
 
     load_field.wait()
     r, c = iota((32, 256), 0), iota((32, 256), 1)
@@ -123,36 +211,48 @@
         cp.start()
         stage1.append(cp)
 
-    def fine_copy(h, i):
-        dz, dy = SIDES[i]
-        vs = pl.ds(h * VCH, VCH)
-        if dy == 0:
-            src = fld.at[vs, pl.ds(192 if dz > 0 else 0, 64)]
-            dst = halo.at[vs, pl.ds(0 if dz > 0 else 64, 64)]
-        elif dz == 0:
-            src = strips.at[1 if dy > 0 else 0, vs]
-            dst = halo.at[vs, pl.ds(128 if dy > 0 else 192, 64)]
-        else:
-            src = strips.at[1 if dy > 0 else 0, vs, pl.ds(48 if dz > 0 else 0, 16)]
-            dst = halo.at[vs, pl.ds(256 + (0 if dz > 0 else 32) + (0 if dy > 0 else 16), 16)]
-        return remote(src, dst, fs.at[h, i], fr.at[h, i], dev(0, dy, dz))
-
-    def coarse_copy(i):
-        dz, dy = SIDES[i]
-        if dy == 0:
-            src, dst = cl.at[:, 1 if dz > 0 else 0], ch.at[:, pl.ds(0 if dz > 0 else 2, 2)]
-        elif dz == 0:
-            src, dst = cl.at[:, :, 1 if dy > 0 else 0], ch.at[:, pl.ds(4 if dy > 0 else 6, 2)]
-        else:
-            src = cl.at[:, 1 if dz > 0 else 0, 1 if dy > 0 else 0]
-            dst = ch.at[:, 8 + (0 if dz > 0 else 2) + (0 if dy > 0 else 1)]
-        return remote(src, dst, cs.at[i], cr.at[i], dev(0, dy, dz))
-
-    fine = [[fine_copy(h, i) for i in range(8)] for h in range(NCH)]
-    coarse = [coarse_copy(i) for i in range(8)]
-    for h in range(NCH):
-        fine[h][0].start()
-        fine[h][1].start()
+    def fine_z(h, i):
+        vs, dz = pl.ds(h * VCH, VCH), 1 - 2 * i
+        src = fld.at[vs, pl.ds(192 - 192 * i, 64)]
+        return remote(src, halo.at[vs, pl.ds(64 * i, 64)], fs.at[h, i], fr.at[h, i], dev(0, 0, dz))
+
+    def fine_y(h, i):
+        vs, dy = pl.ds(h * VCH, VCH), 1 - 2 * i
+        dst = halo.at[vs, pl.ds(128 + 64 * i, 64)]
+        return remote(strips.at[1 - i, vs], dst, fs.at[h, 2 + i], fr.at[h, 2 + i], dev(0, dy, 0))
+
+    def fine_corner(h, i):
+        vs, dy = pl.ds(h * VCH, VCH), 1 - 2 * i
+        dst = halo.at[vs, pl.ds(256 + 32 * i, 32)]
+        return remote(relay.at[1 - i, vs], dst, fs.at[h, 4 + i], fr.at[h, 4 + i], dev(0, dy, 0))
+
+    def coarse_z(i):
+        return remote(cl.at[:, 1 - i], ch.at[:, i], cs.at[i], cr.at[i], dev(0, 0, 1 - 2 * i))
+
+    def coarse_y(i):
+        return remote(cl.at[:, :, 1 - i], ch.at[:, 2 + i], cs.at[2 + i], cr.at[2 + i], dev(0, 1 - 2 * i, 0))
+
+    def coarse_corner(i):
+        src = ch.at[:, pl.ds(0, 2), 1 - i]
+        return remote(src, ch.at[:, 4 + i], cs.at[4 + i], cr.at[4 + i], dev(0, 1 - 2 * i, 0))
+
+    z_copies = [[fine_z(h, i) for i in range(2)] for h in range(NCH)]
+    y_copies = [[fine_y(h, i) for i in range(2)] for h in range(NCH)]
+    corner_copies = [[fine_corner(h, i) for i in range(2)] for h in range(NCH)]
+    coarse_z_copies = [coarse_z(i) for i in range(2)]
+    coarse_y_copies = [coarse_y(i) for i in range(2)]
+    coarse_corner_copies = [coarse_corner(i) for i in range(2)]
+
+    def start(copies):
+        for cp in copies:
+            cp.start()
+
+    def wait(copies):
+        for cp in copies:
+            cp.wait()
+
+    start(z_copies[0])
+    start(z_copies[1])
 
     def cut(p, carry):
         pair = jnp.concatenate([fld[2 * p], fld[2 * p + 1]], axis=1)
@@ -167,13 +267,12 @@
         return carry
 
     lax.fori_loop(0, 8, cut, 0, unroll=4)
-    for i in range(2, 8):
-        fine[0][i].start()
-    for i in range(8):
-        coarse[i].start()
-    for h in range(1, NCH):
-        for i in range(2, 8):
-            fine[h][i].start()
+    start(coarse_z_copies)
+    start(z_copies[2])
+    start(z_copies[3])
+    start(coarse_y_copies)
+    for h in range(NCH):
+        start(y_copies[h])
 
     for cp in stage1:
         cp.wait()
@@ -185,76 +284,17 @@
         cp.start()
         stage2.append(cp)
 
-    load_fine.wait()
-    load_coarse.wait()
-    zmin, zmax = jnp.where(gz > 0, -99, 0), jnp.where(gz < NGZ - 1, 99, 0)
-    ymin, ymax = jnp.where(gy > 0, -99, 0), jnp.where(gy < NGY - 1, 99, 0)
-
-    def zy_weights(taps_ref, zi, yi, zo, yo, side):
-        ok = (zi >= zmin) & (yi >= ymin) & (zi < zmax + side) & (yi < ymax + side)
-        w = taps_at(taps_ref, 0, zi - zo + 4) * taps_at(taps_ref, 1, yi - yo + 4)
-        return hi_lo(jnp.where(ok, w, 0.0))
-
-    o, c = iota((256, 256), 0), iota((256, 256), 1)
-    hi, lo = zy_weights(fine_taps, c >> 4, c & 15, o >> 4, o & 15, 16)
-    wf[0, :, pl.ds(0, 256)] = hi
-    wf[1, :, pl.ds(0, 256)] = lo
-    o, c = iota((256, 320), 0), iota((256, 320), 1)
-    z4, y4, q = (c >> 2) & 3, c & 3, (c >> 4) & 3
-    zi = jnp.where(
-        c < 64, (c >> 4) - 4, jnp.where(c < 128, (c >> 4) + 12, jnp.where(c < 256, (c & 63) >> 2, jnp.where(q < 2, z4 - 4, z4 + 16)))
-    )
-    yi = jnp.where(
-        c < 128, c & 15, jnp.where(c < 192, y4 - 4, jnp.where(c < 256, y4 + 16, jnp.where((q & 1) == 0, y4 - 4, y4 + 16)))
-    )
-    hi, lo = zy_weights(fine_taps, zi, yi, o >> 4, o & 15, 16)
-    wf[0, :, pl.ds(256, 320)] = hi
-    wf[1, :, pl.ds(256, 320)] = lo
-    o, c = iota((256, 256), 0), iota((256, 256), 1)
-    z4, y4, q = (c >> 2) & 3, c & 3, c >> 4
-    first = (q & 1) * 4
-    zi = jnp.where(
-        q < 4, ((q >> 1) << 2) + z4,
-        jnp.where(q < 6, z4 - 4, jnp.where(q < 8, z4 + 8, jnp.where(q < 12, first + z4, jnp.where(q < 14, z4 - 4, z4 + 8)))),
-    )
-    yi = jnp.where(
-        q < 8, first + y4,
-        jnp.where(q < 10, y4 - 4, jnp.where(q < 12, y4 + 8, jnp.where((q & 1) == 0, y4 - 4, y4 + 8))),
-    )
-    hi, lo = zy_weights(coarse_taps, zi, yi, o >> 5, (o & 15) >> 1, 8)
-    wc[0] = hi
-    wc[1] = lo
-
-    k, n = iota((384, 256), 0), iota((384, 256), 1)
-    xo, v = n & 127, n >> 7
-    w = jnp.where(
-        k < 256,
-        jnp.where((k >> 7) == v, taps_at(fine_taps, 2, (k & 127) - xo + 4), 0.0),
-        jnp.where(((k >> 6) & 1) == v, taps_at(coarse_taps, 2, (k & 63) - (xo >> 1) + 4), 0.0),
-    )
-    hi, lo = hi_lo(w)
-    xw[0] = hi
-    xw[1] = lo
-    r, n = iota((32, 256), 0), iota((32, 256), 1)
-    xo, v, e = n & 127, n >> 7, r & 3
-    right = r >= 16
-    w = jnp.where(
-        (r & 8) == 0,
-        taps_at(fine_taps, 2, e + jnp.where(right, 128, -4) - xo + 4),
-        taps_at(coarse_taps, 2, e + jnp.where(right, 64, -4) - (xo >> 1) + 4),
-    )
-    there = jnp.where(right, jnp.where(gx < NGX - 1, 1, 0), jnp.where(gx > 0, 1, 0)) == 1
-    hi, lo = hi_lo(jnp.where(there & (((r >> 2) & 1) == v), w, 0.0))
-    xh[pl.ds(0, 32)] = hi
-    xh[pl.ds(32, 32)] = lo
-
-    for cp in stage2:
-        cp.wait()
-    stage3 = []
-    for d in range(1, NGX):
-        cp = remote(gath.at[gx], gath.at[gx], s3s.at[d - 1], s3r.at[d - 1], dev(d, 0, 0))
-        cp.start()
-        stage3.append(cp)
+    def forward(h):
+        wait(z_copies[h])
+        for p in range(h * PCH, (h + 1) * PCH):
+            pair = [halo[2 * p + v, pl.ds(0, 128)] for v in range(2)]
+            got = nn(rsel, jnp.concatenate(pair, axis=1)).astype(BF16)
+            for v in range(2):
+                for side in range(2):
+                    relay[side, 2 * p + v] = got[side * 32 : side * 32 + 32, v * 128 : v * 128 + 128]
+        start(corner_copies[h])
+
+    forward(0)
 
     load_top.wait()
     k, n = iota((512, 512), 0), iota((512, 512), 1)
@@ -279,12 +319,13 @@
 
     lax.fori_loop(0, 4, reorder, 0)
 
-    r, c = iota((32, 384), 0), iota((32, 384), 1)
-    t, e, right = (r >> 2) & 3, r & 3, r >= 16
-    spot = jnp.where(
-        t < 2, t * 128 + jnp.where(right, 124, 0), 256 + (t & 1) * 64 + jnp.where(right, 60, 0)
-    )
-    pick = jnp.where(c == spot + e, 1.0, 0.0).astype(BF16)
+    for cp in stage2:
+        cp.wait()
+    stage3 = []
+    for d in range(1, NGX):
+        cp = remote(gath.at[gx], gath.at[gx], s3s.at[d - 1], s3r.at[d - 1], dev(d, 0, 0))
+        cp.start()
+        stage3.append(cp)
 
     def zy_pass(p, carry):
         pair = jnp.concatenate([fld[2 * p], fld[2 * p + 1]], axis=1)
@@ -303,29 +344,29 @@
         return carry
 
     edges = []
-    for cp in coarse:
-        cp.wait()
-    for h in range(NCH):
-        for cp in fine[h]:
-            cp.wait()
-        lax.fori_loop(h * PCH, (h + 1) * PCH, zy_pass, 0, unroll=2)
+
+    def zy_chunk(h):
+        wait(y_copies[h])
+        wait(corner_copies[h])
+        for p in range(h * PCH, (h + 1) * PCH):
+            zy_pass(p, 0)
         ps = pl.ds(h * PCH, PCH)
         left = remote(edge_out.at[0, ps], edge_in.at[1, ps], es.at[h, 0], er.at[h, 0], dev(-1, 0, 0))
         right = remote(edge_out.at[1, ps], edge_in.at[0, ps], es.at[h, 1], er.at[h, 1], dev(1, 0, 0))
-        left.start()
-        right.start()
         edges.append((left, right))
-
-    def x_pass(p, carry):
-        both = tt[p]
-        ends = jnp.concatenate([edge_in[0, p], edge_in[1, p]], axis=0)
-        base[p] = nn(both, xw[0]) + nn(both, xw[1]) + tn(jnp.concatenate([ends, ends], axis=0), xh[...])
-        return carry
-
-    for h in range(NCH):
-        for cp in edges[h]:
-            cp.wait()
-        lax.fori_loop(h * PCH, (h + 1) * PCH, x_pass, 0, unroll=2)
+        start(edges[h])
+
+    wait(coarse_z_copies)
+    start(coarse_corner_copies)
+    forward(1)
+    wait(coarse_y_copies)
+    wait(coarse_corner_copies)
+    zy_chunk(0)
+    forward(2)
+    zy_chunk(1)
+    forward(3)
+    zy_chunk(2)
+    zy_chunk(3)
 
     def gather_dot(x):
         tiles = [gath[x, g, half] for g in range(NGY) for half in range(2)]
@@ -342,19 +383,21 @@
     lo2 = (sums - hi.astype(F32) - lo.astype(F32)).astype(BF16)
     prol[...] = tn(hi, spread) + tn(lo, spread) + tn(lo2, spread)
 
-    def finish(p, carry):
-        for v in range(2):
-            for zt in range(2):
-                rows = [
-                    prol[pl.ds(2 * p + v, 1), pl.ds((zt * 2 + yt) * 128, 128)] for yt in range(2)
-                ]
-                block = jnp.concatenate([jnp.broadcast_to(row, (8, 128)) for row in rows], axis=0)
-                for i in range(8):
-                    at = pl.ds((zt * 8 + i) * 16, 16)
-                    out[2 * p + v, at] = (base[p, at, pl.ds(v * 128, 128)] + block).astype(BF16)
-        return carry
-
-    lax.fori_loop(0, 8, finish, 0, unroll=True)
+    for h in range(NCH):
+        wait(edges[h])
+        for p in range(h * PCH, (h + 1) * PCH):
+            both = tt[p]
+            ends = jnp.concatenate([edge_in[0, p], edge_in[1, p]], axis=0)
+            got = nn(both, xw[0]) + nn(both, xw[1]) + tn(jnp.concatenate([ends, ends], axis=0), xh[...])
+            for v in range(2):
+                for zt in range(2):
+                    rows = [
+                        prol[pl.ds(2 * p + v, 1), pl.ds((zt * 2 + yt) * 128, 128)] for yt in range(2)
+                    ]
+                    block = jnp.concatenate([jnp.broadcast_to(row, (8, 128)) for row in rows], axis=0)
+                    block = jnp.concatenate([block] * 8, axis=0)
+                    mine = got[zt * 128 : zt * 128 + 128, v * 128 : v * 128 + 128]
+                    out[2 * p + v, pl.ds(zt * 128, 128)] = (mine + block).astype(BF16)
 
 
 def shards(field, fine_taps, coarse_taps, top_kernel):
@@ -376,11 +419,11 @@
             vm((16, 320, 128), BF16),
             vm((2, 16, 64, 128), BF16),
             vm((8, 2, 2, 16, 128), BF16),
-            vm((8, 12, 16, 128), BF16),
+            vm((8, 6, 2, 16, 128), BF16),
             vm((8, 256, 384), BF16),
             vm((2, 8, 16, 256), BF16),
             vm((2, 8, 16, 256), BF16),
-            vm((8, 256, 256), F32),
+            vm((2, 16, 32, 128), BF16),
             vm((2, 256, 576), BF16),
             vm((2, 256, 256), BF16),
             vm((2, 384, 256), BF16),
@@ -394,8 +437,8 @@
             vm((4, 16, 128), BF16),
             vm((16, 512), F32),
             vm((16, 512), F32),
-            dma((NCH, 8)), dma((NCH, 8)),
-            dma((8,)), dma((8,)),
+            dma((NCH, 6)), dma((NCH, 6)),
+            dma((6,)), dma((6,)),
             dma((NCH, 2)), dma((NCH, 2)),
             dma((3,)), dma((3,)),
             dma((15,)), dma((15,)),

time: 38 us -> 36.6 us (0.963)
  the two profiles are of different devices: /device:TPU:1 before, /device:TPU:6 now
where the time goes in v5:
time: 36.6 us; the launch traced here: 36.5 us
  Pallas kernels  35.5 us (97%)
  local copies, waits for them, and re-layouts  0.97 us (3%)
    pallas_call x1, Pallas kernels, shards(): pl.pallas_call(kernel, name='covariance', out_shape=pltpu.VMEM((16, 256,...  35.5 us
    unnamed x1, local copies, waits for them, and re-layouts  0.97 us

profile of v5, /device:TPU:6, one launch (start us, length us, event | category | flops | bytes accessed | tf_op | source)
XLA Modules:
  0.0 36.5 jit_solution(4861308101248480168)
XLA Ops:
  0.0 35.5 %covariance.1 = bf16[16,256,128]{2,1,0:T(8,128)(2,1)S(1)} custom-call(bf16[16,256,128]{2,1,0:T(8,128)(2,1)} %bitcast.5, f32[3,9]{1,0:T(4,128)} %fine_hbm.1, f32[3,9]{1,0:T(4,128)} %coarse_hbm.1, bf16[64,16384]{1,0:T(8,128)(2,1)} %bitcast.4), custom_call_target="tpu_custom_call" | custom-call | tf_op jit(solution)/shard_map/covariance/pallas_call | solution.py:409
  35.5 1.0 %copy.6 = bf16[16,16,16,128]{3,2,1,0:T(8,128)(2,1)} copy(bf16[16,16,16,128]{3,2,1,0:T(8,128)(2,1)S(1)} %bitcast.3) | data formatting | bytes 2097152

commit v6 on v5

--- a/solution.py
+++ b/solution.py
@@ -49,9 +49,12 @@
     fine_taps, coarse_taps,
     fld, halo, strips, cl, ch, tt, edge_out, edge_in, relay,
     wf, wc, xw, xh, gsel, rx, perm, kv, kp, gath, tile_in, psum, prol,
-    fs, fr, cs, cr, es, er, s1s, s1r, s2s, s2r, s3s, s3r, lsem,
+    fs, fr, cs, cr, es, er, s1s, s1r, s2s, s2r, s3s, s3r, s4s, s4r, lsem,
 ):
     gx, gy, gz = lax.axis_index("gx"), lax.axis_index("gy"), lax.axis_index("gz")
+
+    core = lax.rem(gy, 2)
+    pair = lax.div(gy, 2)
 
     def dev(dx, dy, dz):
         return (
@@ -75,7 +78,7 @@
     load_top.start()
 
     barrier = pltpu.get_barrier_semaphore()
-    partners = [(i, 0, 0) for i in range(1, NGX)] + [(0, i, 0) for i in range(1, NGY)]
+    partners = [(i, 0, 0) for i in range(1, NGX)] + [(0, i, 0) for i in (1, -1, *range(2, NGY, 2))]
     partners += [(0, 0, i) for i in range(1, NGZ)]
     for d in partners:
         pl.semaphore_signal(barrier, inc=1, device_id=dev(*d), device_id_type=MESH)
@@ -271,18 +274,21 @@
     start(z_copies[2])
     start(z_copies[3])
     start(coarse_y_copies)
-    for h in range(NCH):
-        start(y_copies[h])
+    start(y_copies[0])
 
     for cp in stage1:
         cp.wait()
     for half in range(2):
-        gath[gx, gy, half] = tile_in[2 * half] + tile_in[2 * half + 1]
+        gath[gx, pair, core, half] = tile_in[2 * half] + tile_in[2 * half + 1]
     stage2 = []
-    for d in range(1, NGY):
-        cp = remote(gath.at[gx, gy], gath.at[gx, gy], s2s.at[d - 1], s2r.at[d - 1], dev(0, d, 0))
+    for d in range(1, 8):
+        mine = gath.at[gx, pair, core]
+        cp = remote(mine, mine, s2s.at[d - 1], s2r.at[d - 1], dev(0, 2 * d, 0))
         cp.start()
         stage2.append(cp)
+
+    for h in range(1, NCH):
+        start(y_copies[h])
 
     def forward(h):
         wait(z_copies[h])
@@ -319,14 +325,6 @@
 
     lax.fori_loop(0, 4, reorder, 0)
 
-    for cp in stage2:
-        cp.wait()
-    stage3 = []
-    for d in range(1, NGX):
-        cp = remote(gath.at[gx], gath.at[gx], s3s.at[d - 1], s3r.at[d - 1], dev(d, 0, 0))
-        cp.start()
-        stage3.append(cp)
-
     def zy_pass(p, carry):
         pair = jnp.concatenate([fld[2 * p], fld[2 * p + 1]], axis=1)
         near = jnp.concatenate([halo[2 * p], halo[2 * p + 1]], axis=1)
@@ -358,6 +356,25 @@
 
     wait(coarse_z_copies)
     start(coarse_corner_copies)
+    for cp in stage2:
+        cp.wait()
+    stage3 = []
+    for d in range(1, NGX):
+        mine = gath.at[gx, :, core]
+        cp = remote(mine, mine, s3s.at[d - 1], s3r.at[d - 1], dev(d, 0, 0))
+        cp.start()
+        stage3.append(cp)
+    sibling = dev(0, 1 - 2 * core, 0)
+    mine = gath.at[gx, :, core]
+    shared = [remote(mine, mine, s4s.at[0], s4r.at[0], sibling)]
+    shared[0].start()
+
+    def share(d):
+        stage3[d - 1].wait()
+        theirs = gath.at[lax.rem(gx + (NGX - d), NGX), :, core]
+        shared.append(remote(theirs, theirs, s4s.at[d], s4r.at[d], sibling))
+        shared[d].start()
+
     forward(1)
     wait(coarse_y_copies)
     wait(coarse_corner_copies)
@@ -365,16 +382,19 @@
     forward(2)
     zy_chunk(1)
     forward(3)
+    for d in range(1, NGX):
+        share(d)
     zy_chunk(2)
     zy_chunk(3)
 
     def gather_dot(x):
-        tiles = [gath[x, g, half] for g in range(NGY) for half in range(2)]
+        tiles = [gath[x, g // 2, g % 2, half] for g in range(NGY) for half in range(2)]
         return nt(kp[x], jnp.concatenate(tiles, axis=1))
 
+    shared[0].wait()
     sums = gather_dot(gx)
     for d in range(1, NGX):
-        stage3[d - 1].wait()
+        shared[d].wait()
         sums = sums + gather_dot(lax.rem(gx + (NGX - d), NGX))
 
     k, n = iota((64, 512), 0), iota((64, 512), 1)
@@ -433,7 +453,7 @@
             vm((512, 512), BF16),
             vm((64, 16384), BF16),
             vm((4, 64, 4096), BF16),
-            vm((4, 16, 2, 16, 128), BF16),
+            vm((4, 8, 2, 2, 16, 128), BF16),
             vm((4, 16, 128), BF16),
             vm((16, 512), F32),
             vm((16, 512), F32),
@@ -441,8 +461,9 @@
             dma((6,)), dma((6,)),
             dma((NCH, 2)), dma((NCH, 2)),
             dma((3,)), dma((3,)),
-            dma((15,)), dma((15,)),
+            dma((7,)), dma((7,)),
             dma((3,)), dma((3,)),
+            dma((4,)), dma((4,)),
             dma((4,)),
         ],
         compiler_params=pltpu.CompilerParams(

time: 36.6 us -> 32.7 us (0.89)
  the two profiles are of different devices: /device:TPU:6 before, /device:TPU:1 now
where the time goes in v6:
time: 32.7 us; the launch traced here: 32.3 us
  Pallas kernels  31.3 us (96%)
  local copies, waits for them, and re-layouts  0.97 us (3%)
    pallas_call x1, Pallas kernels, shards(): pl.pallas_call(kernel, name='covariance', out_shape=pltpu.VMEM((16, 256,...  31.3 us
    unnamed x1, local copies, waits for them, and re-layouts  0.97 us

profile of v6, /device:TPU:1, one launch (start us, length us, event | category | flops | bytes accessed | tf_op | source)
XLA Modules:
  0.0 32.3 jit_solution(15496648661897671371)
XLA Ops:
  0.0 31.3 %covariance.1 = bf16[16,256,128]{2,1,0:T(8,128)(2,1)S(1)} custom-call(bf16[16,256,128]{2,1,0:T(8,128)(2,1)} %bitcast.5, f32[3,9]{1,0:T(4,128)} %fine_hbm.1, f32[3,9]{1,0:T(4,128)} %coarse_hbm.1, bf16[64,16384]{1,0:T(8,128)(2,1)} %bitcast.4), custom_call_target="tpu_custom_call" | custom-call | tf_op jit(solution)/shard_map/covariance/pallas_call | solution.py:429
  31.3 1.0 %copy.6 = bf16[16,16,16,128]{3,2,1,0:T(8,128)(2,1)} copy(bf16[16,16,16,128]{3,2,1,0:T(8,128)(2,1)S(1)} %bitcast.3) | data formatting | bytes 2097152
